TPU v7x, 32 devices: a whole 2x2x4 slice. The times are simulated.
32 devices in a mesh: section: 4 (over y, core), ep: 8 (over z, x).
Axes of the slice: x: 2, y: 2, z: 4, core: 2. Of those that a mesh axis runs over, the one named last changes fastest.
Arguments:
- rows_in: bfloat16 [4, 64, 7168], P(None, 'ep'), may hold values from -6 to 6
- routes: int32 [4, 4, 64, 2], P('section', None, 'ep'), may hold values from 0 to 3, all different within a row; in each aligned block of 8 rows (0 to 7, 8 to 15, ..., all dimensions but the last counted through in order) at most 4 rows name the same one
- hot_blocks: int32 [4], P('section'), may hold values from 0 to 15
- gains: float32 [4, 7168], P('section'), may hold values from 0.1 to 1.9
- router: bfloat16 [4, 7168, 4], P('section'), may hold values from -0.0625 to 0.0625
- w_gate: bfloat16 [4, 7168, 4096], P('section', None, 'ep'), may hold values from -0.0625 to 0.0625
- w_up: bfloat16 [4, 7168, 4096], P('section', None, 'ep'), may hold values from -0.0625 to 0.0625
- w_down: bfloat16 [4, 4096, 7168], P('section', 'ep'), may hold values from -0.1875 to 0.1875
Outputs:
- section_rows: bfloat16 [4, 4, 64, 7168], P('section', None, 'ep')
- relative_load: float32 [4, 8], P('section', 'ep')
Inputs may be any that keep to these rules, and one draw needn't show every extreme that they name: `routes`: in every layer and micro-batch the 8 rows of one device name each expert at most 4 times.
All inputs are finite; a program needn't handle non-finite values.
Results may differ from a plain program's by a relative error of at most 0.025.
Values may be sent and summed in bfloat16 or wider, within the bound.
A program may use at most 128 MiB of HBM per device.

v0:
```python
import jax
import jax.numpy as jnp
from jax import lax
from jax.sharding import PartitionSpec as P

FFW = 1024
BLK = 256


def spread(block, axis, source):
    block = jnp.where(lax.axis_index(axis) == source, block, jnp.zeros_like(block))
    return lax.psum(block, axis)


def shifted(block, axis, distance):
    devices = range(lax.axis_size(axis))
    route = [(i - distance, i) for i in devices if i - distance in devices]
    return lax.ppermute(block, axis, route)


def local(rows_in, routes, hot_blocks, gains, router, w_gate, w_up, w_down):
    section_index = lax.axis_index("section")
    ep_index = lax.axis_index("ep")
    section_count = lax.axis_size("section")
    micro_count = rows_in.shape[0]
    tok_rows = rows_in.shape[1]
    model_width = rows_in.shape[2]
    columns = w_gate.shape[2]
    expert_count = router.shape[2]
    top_count = routes.shape[3]
    capacity = tok_rows // 2
    blocks_per_expert = FFW // BLK
    hot_index = hot_blocks[0]
    owner_index = hot_index // 2
    hot_expert = hot_index // blocks_per_expert
    norm_gain = gains[0]
    router_w = router[0]
    gate_w = w_gate[0]
    up_w = w_up[0]
    down_w = w_down[0]
    column_block = 2 * ep_index + lax.iota(jnp.int32, columns) // BLK
    keep_column = (column_block != hot_index)[None, :]
    expert_ids = lax.iota(jnp.int32, expert_count)
    block_start = hot_index % 2 * BLK
    copy_gate, copy_up, copy_down = (
        spread(lax.dynamic_slice_in_dim(gate_w, block_start, BLK, 1), "ep", owner_index),
        spread(lax.dynamic_slice_in_dim(up_w, block_start, BLK, 1), "ep", owner_index),
        spread(lax.dynamic_slice_in_dim(down_w, block_start, BLK, 0), "ep", owner_index),
    )

    def expert_rows(flat_rows):
        gate_value = jnp.dot(flat_rows, gate_w, preferred_element_type=jnp.float32)
        up_value = jnp.dot(flat_rows, up_w, preferred_element_type=jnp.float32)
        activation = (jax.nn.silu(gate_value) * up_value).astype(jnp.bfloat16)
        home_act = jnp.where(keep_column, activation, jnp.zeros_like(activation))
        return jnp.dot(home_act, down_w, preferred_element_type=jnp.float32).astype(jnp.bfloat16)

    def work_both(recv_parts):
        recv_rows, recv_flags = recv_parts
        sources = recv_rows.shape[0]
        item_count = recv_rows.shape[1]
        home_part = expert_rows(recv_rows.reshape(sources * item_count, model_width))
        home_part = home_part.reshape(sources, item_count, model_width)
        returned = lax.all_to_all(home_part, "ep", split_axis=0, concat_axis=0, tiled=True)
        filled = jnp.sum(recv_flags.astype(jnp.float32), axis=0, keepdims=True)
        return (returned, filled)

    def apply_layer(layer_input, route_ids):
        rows_float = layer_input.astype(jnp.float32)
        mean_square = jnp.mean(rows_float * rows_float, axis=-1, keepdims=True)
        normed = (rows_float * lax.rsqrt(mean_square + 1e-06) * norm_gain).astype(jnp.bfloat16)
        scores = jax.nn.sigmoid(jnp.dot(normed, router_w, preferred_element_type=jnp.float32))
        member = (route_ids[:, :, None] == expert_ids[None, None, :]).astype(jnp.float32)
        chosen = jnp.sum(member * scores[:, None, :], axis=2)
        gate_weights = 2.5 * chosen / jnp.sum(chosen, axis=1, keepdims=True)
        token_gate = jnp.sum(member * gate_weights[:, :, None], axis=1)
        routed = jnp.sum(member, axis=1)
        slot_rank = jnp.cumsum(routed, axis=0) - routed
        slot_ids = lax.iota(jnp.float32, capacity)
        placement = routed.T[:, None, :] * (
            slot_rank.T[:, None, :] == slot_ids[None, :, None]
        ).astype(jnp.float32)
        packed = jnp.einsum(
            "ect,tf->ecf",
            placement.astype(jnp.bfloat16),
            normed,
            preferred_element_type=jnp.float32,
        ).astype(jnp.bfloat16)
        slot_flags = jnp.sum(placement, axis=2).astype(jnp.bfloat16)
        send_rows = jnp.repeat(packed, 2, axis=0)
        send_flags = jnp.repeat(slot_flags, 2, axis=0)
        home_back, filled = work_both(
            (
                lax.all_to_all(send_rows, "ep", split_axis=0, concat_axis=0, tiled=True),
                lax.all_to_all(send_flags, "ep", split_axis=0, concat_axis=0, tiled=True),
            )
        )
        combined = home_back.astype(jnp.float32).reshape(expert_count, 2, capacity, model_width)
        pair_sum = combined[:, 0] + combined[:, 1]
        weighting = placement * token_gate.T[:, None, :]
        routed_sum = jnp.einsum("ect,ecf->tf", weighting, pair_sum, precision=lax.Precision.HIGHEST)
        local_gate = jnp.dot(normed, copy_gate, preferred_element_type=jnp.float32)
        local_up = jnp.dot(normed, copy_up, preferred_element_type=jnp.float32)
        local_act = (jax.nn.silu(local_gate) * local_up).astype(jnp.bfloat16)
        local_part = (
            jnp.dot(local_act, copy_down, preferred_element_type=jnp.float32)
            .astype(jnp.bfloat16)
            .astype(jnp.float32)
        )
        hot_gate = jnp.sum(jnp.where((expert_ids == hot_expert)[None, :], token_gate, 0.0), axis=1)
        routed_sum = routed_sum + hot_gate[:, None] * local_part
        own_hot = jnp.sum(jnp.where((expert_ids == hot_expert)[None, :], routed, 0.0))
        return ((rows_float + routed_sum).astype(jnp.bfloat16), jnp.sum(filled), own_hot)

    def run_tick(tick_index, loop_state):
        incoming, outputs, home_total, hot_total = loop_state
        micro_index = tick_index - section_index
        is_live = (micro_index >= 0) & (micro_index < micro_count)
        clipped = jnp.clip(micro_index, 0, micro_count - 1)
        fresh_rows = lax.dynamic_index_in_dim(rows_in, clipped, 0, keepdims=False)
        layer_input = jnp.where(section_index == 0, fresh_rows, incoming)
        route_ids = lax.dynamic_index_in_dim(routes[0], clipped, 0, keepdims=False)
        next_rows, home_rows, hot_rows = apply_layer(layer_input, route_ids)
        updated = lax.dynamic_update_index_in_dim(outputs, next_rows, clipped, 0)
        outputs = jnp.where(is_live, updated, outputs)
        home_total = home_total + jnp.where(is_live, home_rows, 0.0)
        hot_total = hot_total + jnp.where(is_live, hot_rows, 0.0)
        incoming = shifted(next_rows, "section", 1)
        return (incoming, outputs, home_total, hot_total)

    tick_count = micro_count + section_count - 1
    start_state = (
        jnp.zeros((tok_rows, model_width), jnp.bfloat16),
        jnp.zeros(rows_in.shape, jnp.bfloat16),
        jnp.float32(0.0),
        jnp.float32(0.0),
    )
    final_state = lax.fori_loop(0, tick_count, run_tick, start_state)
    outputs = final_state[1]
    unit_count = (
        final_state[2] * (2.0 - (owner_index == ep_index).astype(jnp.float32)) + final_state[3]
    )
    relative = unit_count / float(micro_count * tok_rows * top_count * blocks_per_expert)
    return (outputs[None], relative.reshape(1, 1))


def solution(mesh):
    return jax.shard_map(
        local,
        mesh=mesh,
        in_specs=(
            P(None, "ep", None),
            P("section", None, "ep", None),
            P("section"),
            P("section", None),
            P("section", None, None),
            P("section", None, "ep"),
            P("section", None, "ep"),
            P("section", "ep", None),
        ),
        out_specs=(P("section", None, "ep", None), P("section", "ep")),
        check_vma=False,
    )
```

profile of v0, /device:TPU:5, one launch (start us, length us, event | category | flops | bytes accessed | tf_op | source)
XLA Modules:
  0.0 805.3 jit_solution(853677512756800073)
XLA Ops:
  12.7 6.3 select_bitcast_fusion.1
  19.1 342.0 %all-reduce.3.cloned.1.call-done = (bf16[7168,256]{1,0:T(8,128)(2,1)}, bf16[7168,256]{1,0:T(8,128)(2,1)}, bf16[256,7168]{1,0:T(8,128)(2,1)}) async-done(((bf16[7168,256]{1,0:T(8,128)(2,1)}, bf16[7168,256]{1,0:T(8,128)(2,1)}, bf16[256,7168]{1,0:T(8,128)(2,1)}), (bf16[7168,256]{1,0:T(8,128)(2,1)}, bf16[7168,256]{1,0:T(8,128)(2,1)}, bf16[256,7168]{1,0:T(8,128)(2,1)})) %all-reduce.3.cloned.1.call-update) | async-done | bytes 11010064 | tf_op jit(solution)/shard_map/psum | solution.py:12
  361.1 435.4 %while.22 = (s32[]{:T(128)}, bf16[8,7168]{1,0:T(8,128)(2,1)S(1)}, bf16[4,8,7168]{2,1,0:T(8,128)(2,1)S(1)}, f32[]{:T(128)}, f32[]{:T(128)}, /*index=5*/pred[]{:T(...) while((s32[]{:T(128)}, bf16[8,7168]{1,0:T(8,128)(2,1)S(1)}, ...), condition=%wide.region_14.15_spmd.clone.clone, body=%wide.region_3.14_spmd.clone.clone.sunk | while | flops 808455232 | bytes 45640856 | solution.py:138
  369.5 10.9 %all-to-all-done = bf16[8,4,7168]{2,1,0:T(4,128)(2,1)S(1)} async-done(((bf16[8,4,7168]{2,1,0:T(4,128)(2,1)}), bf16[8,4,7168]{2,1,0:T(4,128)(2,1)S(1)}, u32[]{:S(2)}, u32[]{:S(2)}) %all-to-all-start) | async-done | bytes 458784 | tf_op jit(solution)/shard_map/while/body/eval_jaxpr/all_to_all | solution.py:94
  384.9 7.9 convolution_convert_fusion.6
  401.0 5.3 fusion.106
  433.4 7.3 all-to-all-done
  445.3 7.9 convolution_convert_fusion.6
  454.1 7.1 all-to-all-start.1
  463.9 5.3 fusion.106
  474.7 6.0 all-to-all-start.2
  495.5 7.2 all-to-all-done
  507.2 7.9 convolution_convert_fusion.6
  516.1 7.0 all-to-all-start.1
  536.4 6.2 all-to-all-start.2
  557.4 7.2 all-to-all-done
  569.1 7.9 convolution_convert_fusion.6
  577.9 7.0 all-to-all-start.1
  598.2 6.2 all-to-all-start.2
  619.2 7.2 all-to-all-done
  631.0 7.9 convolution_convert_fusion.6
  639.8 7.0 all-to-all-start.1
  649.5 5.3 fusion.106
  660.1 6.2 all-to-all-start.2
  681.1 7.2 all-to-all-done
  692.9 7.9 convolution_convert_fusion.6
  701.7 7.0 all-to-all-start.1
  722.0 6.2 all-to-all-start.2
  743.0 7.2 all-to-all-done
  754.7 7.9 convolution_convert_fusion.6
  763.6 7.0 all-to-all-start.1
  783.8 6.2 all-to-all-start.2
  (243 shorter events, 227.4 us)
Async XLA Ops:
  7.2 353.9 %all-reduce.3.cloned.1.call-start = ((), (), s32[]{:S(2)}) async-start(), calls=%async_computation.3 | async-start | bytes 22020096 | tf_op jit(solution)/shard_map/psum | solution.py:12
  7.9 4.8 copy-start
  19.0 342.1 %copy-start.1 = (f32[1,7168]{1,0:T(1,128)S(1)}, f32[1,7168]{1,0:T(1,128)}, u32[]{:S(2)}) copy-start(f32[1,7168]{1,0:T(1,128)} %param.13) | copy-start | bytes 86020
  19.0 342.1 %copy-start.3 = (bf16[1,7168,4]{1,2,0:T(4,128)(2,1)S(1)}, bf16[1,7168,4]{1,2,0:T(4,128)(2,1)}, u32[]{:S(2)}) copy-start(bf16[1,7168,4]{1,2,0:T(4,128)(2,1)} %param.14) | copy-start | bytes 172036
  364.6 15.8 %all-to-all-start = ((bf16[8,4,7168]{2,1,0:T(4,128)(2,1)}), bf16[8,4,7168]{2,1,0:T(4,128)(2,1)S(1)}, u32[]{:S(2)}, u32[]{:S(2)}) async-start(bf16[8,4,7168]{2,1,0:T(4,128)(2,1)} %bitcast.92), calls=%async_computation | async-start | bytes 917504 | tf_op jit(solution)/shard_map/while/body/eval_jaxpr/all_to_all | solution.py:94
  393.8 17.0 %all-to-all-start.1 = ((bf16[8,4,7168]{2,1,0:T(4,128)(2,1)}), bf16[8,4,7168]{2,1,0:T(4,128)(2,1)S(1)}, u32[]{:S(2)}, u32[]{:S(2)}) async-start(bf16[8,4,7168]{2,1,0:T(4,128)(2,1)} %reshape.177), calls=%async_computation.1 | async-start | bytes 917504 | tf_op jit(solution)/shard_map/while/body/eval_jaxpr/all_to_all | solution.py:64
  412.0 13.2 %collective-permute-start = (bf16[8,7168]{1,0:T(8,128)(2,1)S(1)}, bf16[8,7168]{1,0:T(8,128)(2,1)S(1)}, u32[]{:S(2)}, u32[]{:S(2)}) collective-permute-start(bf16[8,7168]{1,0:T(8,128)(2,1)S(1)} %get-tuple-element.674), channel_id=1, source_target_pairs={{0,8},{8,16},{16,24},{1,9},{9,17},{17,25},{2,10},{10,18},{18,26},{... | collective-permute-start | bytes 344072 | tf_op jit(solution)/shard_map/while/body/eval_jaxpr/ppermute | solution.py:18
  414.1 9.8 %all-to-all-start.2 = ((bf16[8,1,4]{2,1,0:T(2,128)(2,1)}), bf16[8,1,4]{2,1,0:T(2,128)(2,1)S(1)}, u32[]{:S(2)}, u32[]{:S(2)}) async-start(bf16[8,1,4]{2,1,0:T(2,128)(2,1)} %copy.40), calls=%async_computation.2 | async-start | bytes 8192 | tf_op jit(solution)/shard_map/while/body/eval_jaxpr/all_to_all | solution.py:95
  428.6 12.2 %all-to-all-start = ((bf16[8,4,7168]{2,1,0:T(4,128)(2,1)}), bf16[8,4,7168]{2,1,0:T(4,128)(2,1)S(1)}, u32[]{:S(2)}, u32[]{:S(2)}) async-start(bf16[8,4,7168]{2,1,0:T(4,128)(2,1)} %bitcast.92), calls=%async_computation | async-start | bytes 917504 | tf_op jit(solution)/shard_map/while/body/eval_jaxpr/all_to_all | solution.py:94
  454.1 17.3 %all-to-all-start.1 = ((bf16[8,4,7168]{2,1,0:T(4,128)(2,1)}), bf16[8,4,7168]{2,1,0:T(4,128)(2,1)S(1)}, u32[]{:S(2)}, u32[]{:S(2)}) async-start(bf16[8,4,7168]{2,1,0:T(4,128)(2,1)} %reshape.177), calls=%async_computation.1 | async-start | bytes 917504 | tf_op jit(solution)/shard_map/while/body/eval_jaxpr/all_to_all | solution.py:64
  472.6 14.6 %collective-permute-start = (bf16[8,7168]{1,0:T(8,128)(2,1)S(1)}, bf16[8,7168]{1,0:T(8,128)(2,1)S(1)}, u32[]{:S(2)}, u32[]{:S(2)}) collective-permute-start(bf16[8,7168]{1,0:T(8,128)(2,1)S(1)} %get-tuple-element.674), channel_id=1, source_target_pairs={{0,8},{8,16},{16,24},{1,9},{9,17},{17,25},{2,10},{10,18},{18,26},{... | collective-permute-start | bytes 344072 | tf_op jit(solution)/shard_map/while/body/eval_jaxpr/ppermute | solution.py:18
  474.7 11.2 %all-to-all-start.2 = ((bf16[8,1,4]{2,1,0:T(2,128)(2,1)}), bf16[8,1,4]{2,1,0:T(2,128)(2,1)S(1)}, u32[]{:S(2)}, u32[]{:S(2)}) async-start(bf16[8,1,4]{2,1,0:T(2,128)(2,1)} %copy.40), calls=%async_computation.2 | async-start | bytes 8192 | tf_op jit(solution)/shard_map/while/body/eval_jaxpr/all_to_all | solution.py:95
  490.7 12.0 %all-to-all-start = ((bf16[8,4,7168]{2,1,0:T(4,128)(2,1)}), bf16[8,4,7168]{2,1,0:T(4,128)(2,1)S(1)}, u32[]{:S(2)}, u32[]{:S(2)}) async-start(bf16[8,4,7168]{2,1,0:T(4,128)(2,1)} %bitcast.92), calls=%async_computation | async-start | bytes 917504 | tf_op jit(solution)/shard_map/while/body/eval_jaxpr/all_to_all | solution.py:94
  516.1 16.9 %all-to-all-start.1 = ((bf16[8,4,7168]{2,1,0:T(4,128)(2,1)}), bf16[8,4,7168]{2,1,0:T(4,128)(2,1)S(1)}, u32[]{:S(2)}, u32[]{:S(2)}) async-start(bf16[8,4,7168]{2,1,0:T(4,128)(2,1)} %reshape.177), calls=%async_computation.1 | async-start | bytes 917504 | tf_op jit(solution)/shard_map/while/body/eval_jaxpr/all_to_all | solution.py:64
  534.3 14.8 %collective-permute-start = (bf16[8,7168]{1,0:T(8,128)(2,1)S(1)}, bf16[8,7168]{1,0:T(8,128)(2,1)S(1)}, u32[]{:S(2)}, u32[]{:S(2)}) collective-permute-start(bf16[8,7168]{1,0:T(8,128)(2,1)S(1)} %get-tuple-element.674), channel_id=1, source_target_pairs={{0,8},{8,16},{16,24},{1,9},{9,17},{17,25},{2,10},{10,18},{18,26},{... | collective-permute-start | bytes 344072 | tf_op jit(solution)/shard_map/while/body/eval_jaxpr/ppermute | solution.py:18
  536.4 11.5 %all-to-all-start.2 = ((bf16[8,1,4]{2,1,0:T(2,128)(2,1)}), bf16[8,1,4]{2,1,0:T(2,128)(2,1)S(1)}, u32[]{:S(2)}, u32[]{:S(2)}) async-start(bf16[8,1,4]{2,1,0:T(2,128)(2,1)} %copy.40), calls=%async_computation.2 | async-start | bytes 8192 | tf_op jit(solution)/shard_map/while/body/eval_jaxpr/all_to_all | solution.py:95
  552.5 12.0 %all-to-all-start = ((bf16[8,4,7168]{2,1,0:T(4,128)(2,1)}), bf16[8,4,7168]{2,1,0:T(4,128)(2,1)S(1)}, u32[]{:S(2)}, u32[]{:S(2)}) async-start(bf16[8,4,7168]{2,1,0:T(4,128)(2,1)} %bitcast.92), calls=%async_computation | async-start | bytes 917504 | tf_op jit(solution)/shard_map/while/body/eval_jaxpr/all_to_all | solution.py:94
  577.9 16.9 %all-to-all-start.1 = ((bf16[8,4,7168]{2,1,0:T(4,128)(2,1)}), bf16[8,4,7168]{2,1,0:T(4,128)(2,1)S(1)}, u32[]{:S(2)}, u32[]{:S(2)}) async-start(bf16[8,4,7168]{2,1,0:T(4,128)(2,1)} %reshape.177), calls=%async_computation.1 | async-start | bytes 917504 | tf_op jit(solution)/shard_map/while/body/eval_jaxpr/all_to_all | solution.py:64
  596.1 14.8 %collective-permute-start = (bf16[8,7168]{1,0:T(8,128)(2,1)S(1)}, bf16[8,7168]{1,0:T(8,128)(2,1)S(1)}, u32[]{:S(2)}, u32[]{:S(2)}) collective-permute-start(bf16[8,7168]{1,0:T(8,128)(2,1)S(1)} %get-tuple-element.674), channel_id=1, source_target_pairs={{0,8},{8,16},{16,24},{1,9},{9,17},{17,25},{2,10},{10,18},{18,26},{... | collective-permute-start | bytes 344072 | tf_op jit(solution)/shard_map/while/body/eval_jaxpr/ppermute | solution.py:18
  598.2 11.5 %all-to-all-start.2 = ((bf16[8,1,4]{2,1,0:T(2,128)(2,1)}), bf16[8,1,4]{2,1,0:T(2,128)(2,1)S(1)}, u32[]{:S(2)}, u32[]{:S(2)}) async-start(bf16[8,1,4]{2,1,0:T(2,128)(2,1)} %copy.40), calls=%async_computation.2 | async-start | bytes 8192 | tf_op jit(solution)/shard_map/while/body/eval_jaxpr/all_to_all | solution.py:95
  614.4 12.0 %all-to-all-start = ((bf16[8,4,7168]{2,1,0:T(4,128)(2,1)}), bf16[8,4,7168]{2,1,0:T(4,128)(2,1)S(1)}, u32[]{:S(2)}, u32[]{:S(2)}) async-start(bf16[8,4,7168]{2,1,0:T(4,128)(2,1)} %bitcast.92), calls=%async_computation | async-start | bytes 917504 | tf_op jit(solution)/shard_map/while/body/eval_jaxpr/all_to_all | solution.py:94
  639.8 16.9 %all-to-all-start.1 = ((bf16[8,4,7168]{2,1,0:T(4,128)(2,1)}), bf16[8,4,7168]{2,1,0:T(4,128)(2,1)S(1)}, u32[]{:S(2)}, u32[]{:S(2)}) async-start(bf16[8,4,7168]{2,1,0:T(4,128)(2,1)} %reshape.177), calls=%async_computation.1 | async-start | bytes 917504 | tf_op jit(solution)/shard_map/while/body/eval_jaxpr/all_to_all | solution.py:64
  658.0 14.8 %collective-permute-start = (bf16[8,7168]{1,0:T(8,128)(2,1)S(1)}, bf16[8,7168]{1,0:T(8,128)(2,1)S(1)}, u32[]{:S(2)}, u32[]{:S(2)}) collective-permute-start(bf16[8,7168]{1,0:T(8,128)(2,1)S(1)} %get-tuple-element.674), channel_id=1, source_target_pairs={{0,8},{8,16},{16,24},{1,9},{9,17},{17,25},{2,10},{10,18},{18,26},{... | collective-permute-start | bytes 344072 | tf_op jit(solution)/shard_map/while/body/eval_jaxpr/ppermute | solution.py:18
  660.1 11.5 %all-to-all-start.2 = ((bf16[8,1,4]{2,1,0:T(2,128)(2,1)}), bf16[8,1,4]{2,1,0:T(2,128)(2,1)S(1)}, u32[]{:S(2)}, u32[]{:S(2)}) async-start(bf16[8,1,4]{2,1,0:T(2,128)(2,1)} %copy.40), calls=%async_computation.2 | async-start | bytes 8192 | tf_op jit(solution)/shard_map/while/body/eval_jaxpr/all_to_all | solution.py:95
  676.3 12.0 %all-to-all-start = ((bf16[8,4,7168]{2,1,0:T(4,128)(2,1)}), bf16[8,4,7168]{2,1,0:T(4,128)(2,1)S(1)}, u32[]{:S(2)}, u32[]{:S(2)}) async-start(bf16[8,4,7168]{2,1,0:T(4,128)(2,1)} %bitcast.92), calls=%async_computation | async-start | bytes 917504 | tf_op jit(solution)/shard_map/while/body/eval_jaxpr/all_to_all | solution.py:94
  701.7 16.9 %all-to-all-start.1 = ((bf16[8,4,7168]{2,1,0:T(4,128)(2,1)}), bf16[8,4,7168]{2,1,0:T(4,128)(2,1)S(1)}, u32[]{:S(2)}, u32[]{:S(2)}) async-start(bf16[8,4,7168]{2,1,0:T(4,128)(2,1)} %reshape.177), calls=%async_computation.1 | async-start | bytes 917504 | tf_op jit(solution)/shard_map/while/body/eval_jaxpr/all_to_all | solution.py:64
  719.9 14.8 %collective-permute-start = (bf16[8,7168]{1,0:T(8,128)(2,1)S(1)}, bf16[8,7168]{1,0:T(8,128)(2,1)S(1)}, u32[]{:S(2)}, u32[]{:S(2)}) collective-permute-start(bf16[8,7168]{1,0:T(8,128)(2,1)S(1)} %get-tuple-element.674), channel_id=1, source_target_pairs={{0,8},{8,16},{16,24},{1,9},{9,17},{17,25},{2,10},{10,18},{18,26},{... | collective-permute-start | bytes 344072 | tf_op jit(solution)/shard_map/while/body/eval_jaxpr/ppermute | solution.py:18
  722.0 11.5 %all-to-all-start.2 = ((bf16[8,1,4]{2,1,0:T(2,128)(2,1)}), bf16[8,1,4]{2,1,0:T(2,128)(2,1)S(1)}, u32[]{:S(2)}, u32[]{:S(2)}) async-start(bf16[8,1,4]{2,1,0:T(2,128)(2,1)} %copy.40), calls=%async_computation.2 | async-start | bytes 8192 | tf_op jit(solution)/shard_map/while/body/eval_jaxpr/all_to_all | solution.py:95
  738.1 12.0 %all-to-all-start = ((bf16[8,4,7168]{2,1,0:T(4,128)(2,1)}), bf16[8,4,7168]{2,1,0:T(4,128)(2,1)S(1)}, u32[]{:S(2)}, u32[]{:S(2)}) async-start(bf16[8,4,7168]{2,1,0:T(4,128)(2,1)} %bitcast.92), calls=%async_computation | async-start | bytes 917504 | tf_op jit(solution)/shard_map/while/body/eval_jaxpr/all_to_all | solution.py:94
  763.6 16.9 %all-to-all-start.1 = ((bf16[8,4,7168]{2,1,0:T(4,128)(2,1)}), bf16[8,4,7168]{2,1,0:T(4,128)(2,1)S(1)}, u32[]{:S(2)}, u32[]{:S(2)}) async-start(bf16[8,4,7168]{2,1,0:T(4,128)(2,1)} %reshape.177), calls=%async_computation.1 | async-start | bytes 917504 | tf_op jit(solution)/shard_map/while/body/eval_jaxpr/all_to_all | solution.py:64
  781.7 14.8 %collective-permute-start = (bf16[8,7168]{1,0:T(8,128)(2,1)S(1)}, bf16[8,7168]{1,0:T(8,128)(2,1)S(1)}, u32[]{:S(2)}, u32[]{:S(2)}) collective-permute-start(bf16[8,7168]{1,0:T(8,128)(2,1)S(1)} %get-tuple-element.674), channel_id=1, source_target_pairs={{0,8},{8,16},{16,24},{1,9},{9,17},{17,25},{2,10},{10,18},{18,26},{... | collective-permute-start | bytes 344072 | tf_op jit(solution)/shard_map/while/body/eval_jaxpr/ppermute | solution.py:18
  783.8 11.5 %all-to-all-start.2 = ((bf16[8,1,4]{2,1,0:T(2,128)(2,1)}), bf16[8,1,4]{2,1,0:T(2,128)(2,1)S(1)}, u32[]{:S(2)}, u32[]{:S(2)}) async-start(bf16[8,1,4]{2,1,0:T(2,128)(2,1)} %copy.40), calls=%async_computation.2 | async-start | bytes 8192 | tf_op jit(solution)/shard_map/while/body/eval_jaxpr/all_to_all | solution.py:95
  (1 other events, 0.8 us)
Sparse Core Ops, SparseCore 0:
  19.2 341.8 all-reduce.2
where the time goes:
time: 821 us; the launch traced here: 805 us
  waiting for transfers between devices  446 us (54%)
  matrix products  152 us (19%)
  starting transfers between devices  122 us (15%)
  other arithmetic  35.8 us (4%)
  local copies, waits for them, and re-layouts  24.2 us (3%)
  between operations  15.9 us (2%)
  loops' own time  9.39 us (1%)
    psum x1, waiting for transfers between devices, spread(): return lax.psum(block, axis)  342 us
    dot_general x7, matrix products, expert_rows(): jnp.dot(home_act, down_w, preferred_element_type=jnp.float32)  55.2 us
    all_to_all x7, waiting for transfers between devices, apply_layer(): lax.all_to_all(send_rows, 'ep', split_axis=0, concat_axis=0, tiled=True)  54.3 us
    all_to_all x7, starting transfers between devices, work_both(): lax.all_to_all(home_part, 'ep', split_axis=0, concat_axis=0, tiled=True)  46.8 us
    all_to_all x7, starting transfers between devices, apply_layer(): lax.all_to_all(send_flags, 'ep', split_axis=0, concat_axis=0, tiled=True)  41.4 us
    dot_general x7, matrix products, apply_layer(): jnp.dot(local_act, copy_down, preferred_element_type=jnp.float32)  36.9 us
    all_to_all x7, waiting for transfers between devices, apply_layer(): lax.all_to_all(send_flags, 'ep', split_axis=0, concat_axis=0, tiled=True)  33 us
    dot_general x7, matrix products, expert_rows(): gate_value = jnp.dot(flat_rows, gate_w, preferred_element_type=jnp.float32)  31 us
  transfers between devices with their start and end apart: 29, of which 22 were waited for; matrix products, arithmetic and copies ran while one was open for 9% of the time, Pallas kernels for 0%

commit v1 on v0

v1 whole, which is shorter than its diff:
```python
import jax
import jax.numpy as jnp
from jax import lax
from jax.sharding import PartitionSpec as P

FFW = 1024
BLK = 256


def shifted(block, axis, distance):
    devices = range(lax.axis_size(axis))
    route = [(i - distance, i) for i in devices if i - distance in devices]
    return lax.ppermute(block, axis, route)


def local(rows_in, routes, hot_blocks, gains, router, w_gate, w_up, w_down):
    section_index = lax.axis_index("section")
    ep_index = lax.axis_index("ep")
    section_count = lax.axis_size("section")
    micro_count = rows_in.shape[0]
    tok_rows = rows_in.shape[1]
    model_width = rows_in.shape[2]
    expert_count = router.shape[2]
    top_count = routes.shape[3]
    capacity = tok_rows // 2
    blocks_per_expert = FFW // BLK
    hot_index = hot_blocks[0]
    owner_index = hot_index // 2
    hot_expert = hot_index // blocks_per_expert
    norm_gain = gains[0]
    router_w = router[0]
    gate_w = w_gate[0]
    up_w = w_up[0]
    down_w = w_down[0]
    expert_ids = lax.iota(jnp.int32, expert_count)

    route_member = (routes[0][..., None] == expert_ids).astype(jnp.float32)
    expert_local = jnp.sum(route_member, axis=(0, 1, 2))
    expert_total = lax.psum(expert_local, "ep")
    own_expert = ep_index // 2
    home_units = jnp.sum(jnp.where(expert_ids == own_expert, expert_total, 0.0))
    own_hot = jnp.sum(jnp.where(expert_ids == hot_expert, expert_local, 0.0))

    def expert_rows(flat_rows):
        gate_value = jnp.dot(flat_rows, gate_w, preferred_element_type=jnp.float32)
        up_value = jnp.dot(flat_rows, up_w, preferred_element_type=jnp.float32)
        activation = (jax.nn.silu(gate_value) * up_value).astype(jnp.bfloat16)
        return jnp.dot(activation, down_w, preferred_element_type=jnp.float32).astype(jnp.bfloat16)

    def apply_layer(layer_input, route_ids):
        rows_float = layer_input.astype(jnp.float32)
        mean_square = jnp.mean(rows_float * rows_float, axis=-1, keepdims=True)
        normed = (rows_float * lax.rsqrt(mean_square + 1e-06) * norm_gain).astype(jnp.bfloat16)
        scores = jax.nn.sigmoid(jnp.dot(normed, router_w, preferred_element_type=jnp.float32))
        member = (route_ids[:, :, None] == expert_ids[None, None, :]).astype(jnp.float32)
        chosen = jnp.sum(member * scores[:, None, :], axis=2)
        gate_weights = 2.5 * chosen / jnp.sum(chosen, axis=1, keepdims=True)
        token_gate = jnp.sum(member * gate_weights[:, :, None], axis=1)
        routed = jnp.sum(member, axis=1)
        slot_rank = jnp.cumsum(routed, axis=0) - routed
        slot_ids = lax.iota(jnp.float32, capacity)
        placement = routed.T[:, None, :] * (
            slot_rank.T[:, None, :] == slot_ids[None, :, None]
        ).astype(jnp.float32)
        packed = jnp.einsum(
            "ect,tf->ecf",
            placement.astype(jnp.bfloat16),
            normed,
            preferred_element_type=jnp.float32,
        ).astype(jnp.bfloat16)
        send_rows = jnp.repeat(packed, 2, axis=0)
        recv_rows = lax.all_to_all(send_rows, "ep", split_axis=0, concat_axis=0, tiled=True)
        sources = recv_rows.shape[0]
        item_count = recv_rows.shape[1]
        part = expert_rows(recv_rows.reshape(sources * item_count, model_width))
        part = part.reshape(sources, item_count, model_width)
        home_back = lax.all_to_all(part, "ep", split_axis=0, concat_axis=0, tiled=True)
        combined = home_back.astype(jnp.float32).reshape(expert_count, 2, capacity, model_width)
        pair_sum = combined[:, 0] + combined[:, 1]
        weighting = placement * token_gate.T[:, None, :]
        routed_sum = jnp.einsum("ect,ecf->tf", weighting, pair_sum, precision=lax.Precision.HIGHEST)
        return (rows_float + routed_sum).astype(jnp.bfloat16)

    def run_tick(tick_index, loop_state):
        incoming, outputs = loop_state
        micro_index = tick_index - section_index
        is_live = (micro_index >= 0) & (micro_index < micro_count)
        clipped = jnp.clip(micro_index, 0, micro_count - 1)
        fresh_rows = lax.dynamic_index_in_dim(rows_in, clipped, 0, keepdims=False)
        layer_input = jnp.where(section_index == 0, fresh_rows, incoming)
        route_ids = lax.dynamic_index_in_dim(routes[0], clipped, 0, keepdims=False)
        next_rows = apply_layer(layer_input, route_ids)
        updated = lax.dynamic_update_index_in_dim(outputs, next_rows, clipped, 0)
        outputs = jnp.where(is_live, updated, outputs)
        incoming = shifted(next_rows, "section", 1)
        return (incoming, outputs)

    tick_count = micro_count + section_count - 1
    start_state = (
        jnp.zeros((tok_rows, model_width), jnp.bfloat16),
        jnp.zeros(rows_in.shape, jnp.bfloat16),
    )
    final_state = lax.fori_loop(0, tick_count, run_tick, start_state)
    outputs = final_state[1]
    unit_count = home_units * (2.0 - (owner_index == ep_index).astype(jnp.float32)) + own_hot
    relative = unit_count / float(micro_count * tok_rows * top_count * blocks_per_expert)
    return (outputs[None], relative.reshape(1, 1))


def solution(mesh):
    return jax.shard_map(
        local,
        mesh=mesh,
        in_specs=(
            P(None, "ep", None),
            P("section", None, "ep", None),
            P("section"),
            P("section", None),
            P("section", None, None),
            P("section", None, "ep"),
            P("section", None, "ep"),
            P("section", "ep", None),
        ),
        out_specs=(P("section", None, "ep", None), P("section", "ep")),
        check_vma=False,
    )
```

time: 821 us -> 416 us (0.51)
  the two profiles are of different devices: /device:TPU:5 before, /device:TPU:0 now
where the time goes in v1:
time: 416 us; the launch traced here: 413 us
  blocking collectives  142 us (34%)
  matrix products  108 us (26%)
  waiting for transfers between devices  96.7 us (23%)
  starting transfers between devices  35.3 us (8%)
  local copies, waits for them, and re-layouts  13.8 us (3%)
  other arithmetic  12.6 us (3%)
    all_to_all x7, blocking collectives, apply_layer(): lax.all_to_all(send_rows, 'ep', split_axis=0, concat_axis=0, tiled=True)  119 us
    all_to_all x7, waiting for transfers between devices, apply_layer(): lax.all_to_all(part, 'ep', split_axis=0, concat_axis=0, tiled=True)  90.1 us
    dot_general x7, matrix products, expert_rows(): jnp.dot(activation, down_w, preferred_element_type=jnp.float32)  55.2 us
    dot_general x7, matrix products, expert_rows(): gate_value = jnp.dot(flat_rows, gate_w, preferred_element_type=jnp.float32)  31 us
    all_to_all x7, starting transfers between devices, apply_layer(): lax.all_to_all(part, 'ep', split_axis=0, concat_axis=0, tiled=True)  26.1 us
    psum x1, blocking collectives, local(): expert_total = lax.psum(expert_local, 'ep')  23.1 us
    ppermute x7, starting transfers between devices, shifted(): return lax.ppermute(block, axis, route)  9.27 us
  transfers between devices with their start and end apart: 14, of which 14 were waited for; matrix products, arithmetic and copies ran while one was open for 0% of the time, Pallas kernels for 0%

profile of v1, /device:TPU:0, one launch (start us, length us, event | category | flops | bytes accessed | tf_op | source)
XLA Modules:
  0.0 413.2 jit_solution(7937424765398039121)
XLA Ops:
  2.7 23.1 %psum.7 = f32[4]{0:T(128)S(1)} all-reduce(f32[4]{0:T(128)S(1)} %convert_reduce_fusion), channel_id=1, replica_groups=mesh['section'=4,'ep'=8] {'ep'}, use_global_device_ids=true, to_apply=%region_9.10 | all-reduce | flops 4 | bytes 32 | tf_op jit(solution)/shard_map/psum | solution.py:39
  27.8 383.5 %while.17 = (s32[]{:T(128)}, bf16[8,7168]{1,0:T(8,128)(2,1)S(1)}, bf16[4,8,7168]{2,1,0:T(8,128)(2,1)S(1)}, pred[]{:T(512)}, s32[]{:T(128)}, /*index=5*/bf16[4,8,...) while((s32[]{:T(128)}, bf16[8,7168]{1,0:T(8,128)(2,1)S(1)}, ...), condition=%wide.region_7.8_spmd.clone, body=%wide.region_0.7_spmd.clone.sunk | while | flops 719652352 | bytes 33399696 | solution.py:103
  32.1 12.3 %all_to_all.24 = bf16[8,4,7168]{2,1,0:T(4,128)(2,1)S(1)} all-to-all(bf16[8,4,7168]{2,1,0:T(4,128)(2,1)S(1)} %bitcast.84), channel_id=1, replica_groups=mesh['section'=4,'ep'=8] {'ep'}, dimensions={0} | all-to-all | bytes 917504 | tf_op jit(solution)/shard_map/while/body/eval_jaxpr/all_to_all | solution.py:72
  44.5 4.4 %fusion.70 = f32[32,512]{1,0:T(8,128)S(1)} fusion(bf16[32,7168]{1,0:T(8,128)(2,1)S(1)} %reshape.98, bf16[7168,512]{1,0:T(8,128)(2,1)} %get-tuple-element.445), kind=kOutput, calls=%fused_computation.57.clone.1 | convolution fusion | flops 234881024 | bytes 7864320 | tf_op jit(solution)/shard_map/while/body/eval_jaxpr/dot_general | solution.py:45
  48.9 7.9 %convolution_convert_fusion.5 = bf16[32,7168]{1,0:T(8,128)(2,1)S(1)} fusion(bf16[512,7168]{1,0:T(8,128)(2,1)} %get-tuple-element.447, bf16[32,7168]{1,0:T(8,128)(2,1)S(1)} %reshape.98, bf16[7168,512]{1,0:T(8,128)(2,1)} %get-tuple-element.446, f32[32,512]{1,0:T(8,128)S(1)} %fusion.70), kind=kOutput, calls=%fused_computation.1.clone.1 | convolution fusion | flops 470089728 | bytes 15663104 | tf_op jit(solution)/shard_map/while/body/eval_jaxpr/dot_general | solution.py:48
  61.3 9.6 %all-to-all-done.1 = bf16[8,4,7168]{2,1,0:T(4,128)(2,1)S(1)} async-done(((bf16[8,4,7168]{2,1,0:T(4,128)(2,1)}), bf16[8,4,7168]{2,1,0:T(4,128)(2,1)S(1)}, u32[]{:S(2)}, u32[]{:S(2)}) %all-to-all-start.1) | async-done | bytes 458784 | tf_op jit(solution)/shard_map/while/body/eval_jaxpr/all_to_all | solution.py:77
  78.6 16.4 %all_to_all.24 = bf16[8,4,7168]{2,1,0:T(4,128)(2,1)S(1)} all-to-all(bf16[8,4,7168]{2,1,0:T(4,128)(2,1)S(1)} %bitcast.84), channel_id=1, replica_groups=mesh['section'=4,'ep'=8] {'ep'}, dimensions={0} | all-to-all | bytes 917504 | tf_op jit(solution)/shard_map/while/body/eval_jaxpr/all_to_all | solution.py:72
  95.1 4.4 %fusion.70 = f32[32,512]{1,0:T(8,128)S(1)} fusion(bf16[32,7168]{1,0:T(8,128)(2,1)S(1)} %reshape.98, bf16[7168,512]{1,0:T(8,128)(2,1)} %get-tuple-element.445), kind=kOutput, calls=%fused_computation.57.clone.1 | convolution fusion | flops 234881024 | bytes 7864320 | tf_op jit(solution)/shard_map/while/body/eval_jaxpr/dot_general | solution.py:45
  99.5 7.9 %convolution_convert_fusion.5 = bf16[32,7168]{1,0:T(8,128)(2,1)S(1)} fusion(bf16[512,7168]{1,0:T(8,128)(2,1)} %get-tuple-element.447, bf16[32,7168]{1,0:T(8,128)(2,1)S(1)} %reshape.98, bf16[7168,512]{1,0:T(8,128)(2,1)} %get-tuple-element.446, f32[32,512]{1,0:T(8,128)S(1)} %fusion.70), kind=kOutput, calls=%fused_computation.1.clone.1 | convolution fusion | flops 470089728 | bytes 15663104 | tf_op jit(solution)/shard_map/while/body/eval_jaxpr/dot_general | solution.py:48
  108.3 4.4 %all-to-all-start.1 = ((bf16[8,4,7168]{2,1,0:T(4,128)(2,1)}), bf16[8,4,7168]{2,1,0:T(4,128)(2,1)S(1)}, u32[]{:S(2)}, u32[]{:S(2)}) async-start(bf16[8,4,7168]{2,1,0:T(4,128)(2,1)} %reshape.99), calls=%async_computation.1 | async-start | bytes 917504 | tf_op jit(solution)/shard_map/while/body/eval_jaxpr/all_to_all | solution.py:77
  112.7 14.0 %all-to-all-done.1 = bf16[8,4,7168]{2,1,0:T(4,128)(2,1)S(1)} async-done(((bf16[8,4,7168]{2,1,0:T(4,128)(2,1)}), bf16[8,4,7168]{2,1,0:T(4,128)(2,1)S(1)}, u32[]{:S(2)}, u32[]{:S(2)}) %all-to-all-start.1) | async-done | bytes 458784 | tf_op jit(solution)/shard_map/while/body/eval_jaxpr/all_to_all | solution.py:77
  134.7 18.0 %all_to_all.24 = bf16[8,4,7168]{2,1,0:T(4,128)(2,1)S(1)} all-to-all(bf16[8,4,7168]{2,1,0:T(4,128)(2,1)S(1)} %bitcast.84), channel_id=1, replica_groups=mesh['section'=4,'ep'=8] {'ep'}, dimensions={0} | all-to-all | bytes 917504 | tf_op jit(solution)/shard_map/while/body/eval_jaxpr/all_to_all | solution.py:72
  152.7 4.4 %fusion.70 = f32[32,512]{1,0:T(8,128)S(1)} fusion(bf16[32,7168]{1,0:T(8,128)(2,1)S(1)} %reshape.98, bf16[7168,512]{1,0:T(8,128)(2,1)} %get-tuple-element.445), kind=kOutput, calls=%fused_computation.57.clone.1 | convolution fusion | flops 234881024 | bytes 7864320 | tf_op jit(solution)/shard_map/while/body/eval_jaxpr/dot_general | solution.py:45
  157.2 7.9 %convolution_convert_fusion.5 = bf16[32,7168]{1,0:T(8,128)(2,1)S(1)} fusion(bf16[512,7168]{1,0:T(8,128)(2,1)} %get-tuple-element.447, bf16[32,7168]{1,0:T(8,128)(2,1)S(1)} %reshape.98, bf16[7168,512]{1,0:T(8,128)(2,1)} %get-tuple-element.446, f32[32,512]{1,0:T(8,128)S(1)} %fusion.70), kind=kOutput, calls=%fused_computation.1.clone.1 | convolution fusion | flops 470089728 | bytes 15663104 | tf_op jit(solution)/shard_map/while/body/eval_jaxpr/dot_general | solution.py:48
  169.6 13.3 %all-to-all-done.1 = bf16[8,4,7168]{2,1,0:T(4,128)(2,1)S(1)} async-done(((bf16[8,4,7168]{2,1,0:T(4,128)(2,1)}), bf16[8,4,7168]{2,1,0:T(4,128)(2,1)S(1)}, u32[]{:S(2)}, u32[]{:S(2)}) %all-to-all-start.1) | async-done | bytes 458784 | tf_op jit(solution)/shard_map/while/body/eval_jaxpr/all_to_all | solution.py:77
  190.7 18.2 %all_to_all.24 = bf16[8,4,7168]{2,1,0:T(4,128)(2,1)S(1)} all-to-all(bf16[8,4,7168]{2,1,0:T(4,128)(2,1)S(1)} %bitcast.84), channel_id=1, replica_groups=mesh['section'=4,'ep'=8] {'ep'}, dimensions={0} | all-to-all | bytes 917504 | tf_op jit(solution)/shard_map/while/body/eval_jaxpr/all_to_all | solution.py:72
  209.0 4.4 %fusion.70 = f32[32,512]{1,0:T(8,128)S(1)} fusion(bf16[32,7168]{1,0:T(8,128)(2,1)S(1)} %reshape.98, bf16[7168,512]{1,0:T(8,128)(2,1)} %get-tuple-element.445), kind=kOutput, calls=%fused_computation.57.clone.1 | convolution fusion | flops 234881024 | bytes 7864320 | tf_op jit(solution)/shard_map/while/body/eval_jaxpr/dot_general | solution.py:45
  213.4 7.9 %convolution_convert_fusion.5 = bf16[32,7168]{1,0:T(8,128)(2,1)S(1)} fusion(bf16[512,7168]{1,0:T(8,128)(2,1)} %get-tuple-element.447, bf16[32,7168]{1,0:T(8,128)(2,1)S(1)} %reshape.98, bf16[7168,512]{1,0:T(8,128)(2,1)} %get-tuple-element.446, f32[32,512]{1,0:T(8,128)S(1)} %fusion.70), kind=kOutput, calls=%fused_computation.1.clone.1 | convolution fusion | flops 470089728 | bytes 15663104 | tf_op jit(solution)/shard_map/while/body/eval_jaxpr/dot_general | solution.py:48
  222.2 3.6 all-to-all-start.1
  225.9 13.3 %all-to-all-done.1 = bf16[8,4,7168]{2,1,0:T(4,128)(2,1)S(1)} async-done(((bf16[8,4,7168]{2,1,0:T(4,128)(2,1)}), bf16[8,4,7168]{2,1,0:T(4,128)(2,1)S(1)}, u32[]{:S(2)}, u32[]{:S(2)}) %all-to-all-start.1) | async-done | bytes 458784 | tf_op jit(solution)/shard_map/while/body/eval_jaxpr/all_to_all | solution.py:77
  246.9 18.2 %all_to_all.24 = bf16[8,4,7168]{2,1,0:T(4,128)(2,1)S(1)} all-to-all(bf16[8,4,7168]{2,1,0:T(4,128)(2,1)S(1)} %bitcast.84), channel_id=1, replica_groups=mesh['section'=4,'ep'=8] {'ep'}, dimensions={0} | all-to-all | bytes 917504 | tf_op jit(solution)/shard_map/while/body/eval_jaxpr/all_to_all | solution.py:72
  265.2 4.4 %fusion.70 = f32[32,512]{1,0:T(8,128)S(1)} fusion(bf16[32,7168]{1,0:T(8,128)(2,1)S(1)} %reshape.98, bf16[7168,512]{1,0:T(8,128)(2,1)} %get-tuple-element.445), kind=kOutput, calls=%fused_computation.57.clone.1 | convolution fusion | flops 234881024 | bytes 7864320 | tf_op jit(solution)/shard_map/while/body/eval_jaxpr/dot_general | solution.py:45
  269.6 7.9 %convolution_convert_fusion.5 = bf16[32,7168]{1,0:T(8,128)(2,1)S(1)} fusion(bf16[512,7168]{1,0:T(8,128)(2,1)} %get-tuple-element.447, bf16[32,7168]{1,0:T(8,128)(2,1)S(1)} %reshape.98, bf16[7168,512]{1,0:T(8,128)(2,1)} %get-tuple-element.446, f32[32,512]{1,0:T(8,128)S(1)} %fusion.70), kind=kOutput, calls=%fused_computation.1.clone.1 | convolution fusion | flops 470089728 | bytes 15663104 | tf_op jit(solution)/shard_map/while/body/eval_jaxpr/dot_general | solution.py:48
  282.1 13.3 %all-to-all-done.1 = bf16[8,4,7168]{2,1,0:T(4,128)(2,1)S(1)} async-done(((bf16[8,4,7168]{2,1,0:T(4,128)(2,1)}), bf16[8,4,7168]{2,1,0:T(4,128)(2,1)S(1)}, u32[]{:S(2)}, u32[]{:S(2)}) %all-to-all-start.1) | async-done | bytes 458784 | tf_op jit(solution)/shard_map/while/body/eval_jaxpr/all_to_all | solution.py:77
  303.1 18.2 %all_to_all.24 = bf16[8,4,7168]{2,1,0:T(4,128)(2,1)S(1)} all-to-all(bf16[8,4,7168]{2,1,0:T(4,128)(2,1)S(1)} %bitcast.84), channel_id=1, replica_groups=mesh['section'=4,'ep'=8] {'ep'}, dimensions={0} | all-to-all | bytes 917504 | tf_op jit(solution)/shard_map/while/body/eval_jaxpr/all_to_all | solution.py:72
  321.4 4.4 %fusion.70 = f32[32,512]{1,0:T(8,128)S(1)} fusion(bf16[32,7168]{1,0:T(8,128)(2,1)S(1)} %reshape.98, bf16[7168,512]{1,0:T(8,128)(2,1)} %get-tuple-element.445), kind=kOutput, calls=%fused_computation.57.clone.1 | convolution fusion | flops 234881024 | bytes 7864320 | tf_op jit(solution)/shard_map/while/body/eval_jaxpr/dot_general | solution.py:45
  325.8 7.9 %convolution_convert_fusion.5 = bf16[32,7168]{1,0:T(8,128)(2,1)S(1)} fusion(bf16[512,7168]{1,0:T(8,128)(2,1)} %get-tuple-element.447, bf16[32,7168]{1,0:T(8,128)(2,1)S(1)} %reshape.98, bf16[7168,512]{1,0:T(8,128)(2,1)} %get-tuple-element.446, f32[32,512]{1,0:T(8,128)S(1)} %fusion.70), kind=kOutput, calls=%fused_computation.1.clone.1 | convolution fusion | flops 470089728 | bytes 15663104 | tf_op jit(solution)/shard_map/while/body/eval_jaxpr/dot_general | solution.py:48
  338.3 13.3 %all-to-all-done.1 = bf16[8,4,7168]{2,1,0:T(4,128)(2,1)S(1)} async-done(((bf16[8,4,7168]{2,1,0:T(4,128)(2,1)}), bf16[8,4,7168]{2,1,0:T(4,128)(2,1)S(1)}, u32[]{:S(2)}, u32[]{:S(2)}) %all-to-all-start.1) | async-done | bytes 458784 | tf_op jit(solution)/shard_map/while/body/eval_jaxpr/all_to_all | solution.py:77
  359.4 18.2 %all_to_all.24 = bf16[8,4,7168]{2,1,0:T(4,128)(2,1)S(1)} all-to-all(bf16[8,4,7168]{2,1,0:T(4,128)(2,1)S(1)} %bitcast.84), channel_id=1, replica_groups=mesh['section'=4,'ep'=8] {'ep'}, dimensions={0} | all-to-all | bytes 917504 | tf_op jit(solution)/shard_map/while/body/eval_jaxpr/all_to_all | solution.py:72
  377.6 4.4 %fusion.70 = f32[32,512]{1,0:T(8,128)S(1)} fusion(bf16[32,7168]{1,0:T(8,128)(2,1)S(1)} %reshape.98, bf16[7168,512]{1,0:T(8,128)(2,1)} %get-tuple-element.445), kind=kOutput, calls=%fused_computation.57.clone.1 | convolution fusion | flops 234881024 | bytes 7864320 | tf_op jit(solution)/shard_map/while/body/eval_jaxpr/dot_general | solution.py:45
  382.0 7.9 %convolution_convert_fusion.5 = bf16[32,7168]{1,0:T(8,128)(2,1)S(1)} fusion(bf16[512,7168]{1,0:T(8,128)(2,1)} %get-tuple-element.447, bf16[32,7168]{1,0:T(8,128)(2,1)S(1)} %reshape.98, bf16[7168,512]{1,0:T(8,128)(2,1)} %get-tuple-element.446, f32[32,512]{1,0:T(8,128)S(1)} %fusion.70), kind=kOutput, calls=%fused_computation.1.clone.1 | convolution fusion | flops 470089728 | bytes 15663104 | tf_op jit(solution)/shard_map/while/body/eval_jaxpr/dot_general | solution.py:48
  394.5 13.3 %all-to-all-done.1 = bf16[8,4,7168]{2,1,0:T(4,128)(2,1)S(1)} async-done(((bf16[8,4,7168]{2,1,0:T(4,128)(2,1)}), bf16[8,4,7168]{2,1,0:T(4,128)(2,1)S(1)}, u32[]{:S(2)}, u32[]{:S(2)}) %all-to-all-start.1) | async-done | bytes 458784 | tf_op jit(solution)/shard_map/while/body/eval_jaxpr/all_to_all | solution.py:77
  (145 shorter events, 82.1 us)
Async XLA Ops:
  57.8 13.1 %all-to-all-start.1 = ((bf16[8,4,7168]{2,1,0:T(4,128)(2,1)}), bf16[8,4,7168]{2,1,0:T(4,128)(2,1)S(1)}, u32[]{:S(2)}, u32[]{:S(2)}) async-start(bf16[8,4,7168]{2,1,0:T(4,128)(2,1)} %reshape.99), calls=%async_computation.1 | async-start | bytes 917504 | tf_op jit(solution)/shard_map/while/body/eval_jaxpr/all_to_all | solution.py:77
  72.1 2.2 collective-permute-start
  108.3 18.4 %all-to-all-start.1 = ((bf16[8,4,7168]{2,1,0:T(4,128)(2,1)}), bf16[8,4,7168]{2,1,0:T(4,128)(2,1)S(1)}, u32[]{:S(2)}, u32[]{:S(2)}) async-start(bf16[8,4,7168]{2,1,0:T(4,128)(2,1)} %reshape.99), calls=%async_computation.1 | async-start | bytes 917504 | tf_op jit(solution)/shard_map/while/body/eval_jaxpr/all_to_all | solution.py:77
  127.9 2.4 collective-permute-start
  166.0 17.0 %all-to-all-start.1 = ((bf16[8,4,7168]{2,1,0:T(4,128)(2,1)}), bf16[8,4,7168]{2,1,0:T(4,128)(2,1)S(1)}, u32[]{:S(2)}, u32[]{:S(2)}) async-start(bf16[8,4,7168]{2,1,0:T(4,128)(2,1)} %reshape.99), calls=%async_computation.1 | async-start | bytes 917504 | tf_op jit(solution)/shard_map/while/body/eval_jaxpr/all_to_all | solution.py:77
  184.2 2.2 collective-permute-start
  222.2 17.0 %all-to-all-start.1 = ((bf16[8,4,7168]{2,1,0:T(4,128)(2,1)}), bf16[8,4,7168]{2,1,0:T(4,128)(2,1)S(1)}, u32[]{:S(2)}, u32[]{:S(2)}) async-start(bf16[8,4,7168]{2,1,0:T(4,128)(2,1)} %reshape.99), calls=%async_computation.1 | async-start | bytes 917504 | tf_op jit(solution)/shard_map/while/body/eval_jaxpr/all_to_all | solution.py:77
  240.4 2.2 collective-permute-start
  278.4 17.0 %all-to-all-start.1 = ((bf16[8,4,7168]{2,1,0:T(4,128)(2,1)}), bf16[8,4,7168]{2,1,0:T(4,128)(2,1)S(1)}, u32[]{:S(2)}, u32[]{:S(2)}) async-start(bf16[8,4,7168]{2,1,0:T(4,128)(2,1)} %reshape.99), calls=%async_computation.1 | async-start | bytes 917504 | tf_op jit(solution)/shard_map/while/body/eval_jaxpr/all_to_all | solution.py:77
  296.6 2.2 collective-permute-start
  334.7 17.0 %all-to-all-start.1 = ((bf16[8,4,7168]{2,1,0:T(4,128)(2,1)}), bf16[8,4,7168]{2,1,0:T(4,128)(2,1)S(1)}, u32[]{:S(2)}, u32[]{:S(2)}) async-start(bf16[8,4,7168]{2,1,0:T(4,128)(2,1)} %reshape.99), calls=%async_computation.1 | async-start | bytes 917504 | tf_op jit(solution)/shard_map/while/body/eval_jaxpr/all_to_all | solution.py:77
  352.9 2.2 collective-permute-start
  390.9 17.0 %all-to-all-start.1 = ((bf16[8,4,7168]{2,1,0:T(4,128)(2,1)}), bf16[8,4,7168]{2,1,0:T(4,128)(2,1)S(1)}, u32[]{:S(2)}, u32[]{:S(2)}) async-start(bf16[8,4,7168]{2,1,0:T(4,128)(2,1)} %reshape.99), calls=%async_computation.1 | async-start | bytes 917504 | tf_op jit(solution)/shard_map/while/body/eval_jaxpr/all_to_all | solution.py:77
  409.1 2.2 collective-permute-start
  411.3 0.8 copy-start

commit v2 on v1

--- a/solution.py
+++ b/solution.py
@@ -52,22 +52,23 @@
         mean_square = jnp.mean(rows_float * rows_float, axis=-1, keepdims=True)
         normed = (rows_float * lax.rsqrt(mean_square + 1e-06) * norm_gain).astype(jnp.bfloat16)
         scores = jax.nn.sigmoid(jnp.dot(normed, router_w, preferred_element_type=jnp.float32))
-        member = (route_ids[:, :, None] == expert_ids[None, None, :]).astype(jnp.float32)
-        chosen = jnp.sum(member * scores[:, None, :], axis=2)
-        gate_weights = 2.5 * chosen / jnp.sum(chosen, axis=1, keepdims=True)
-        token_gate = jnp.sum(member * gate_weights[:, :, None], axis=1)
-        routed = jnp.sum(member, axis=1)
-        slot_rank = jnp.cumsum(routed, axis=0) - routed
+        member = (route_ids[..., None] == expert_ids).astype(jnp.float32)
+        chosen = jnp.sum(member * scores[:, :, None, :], axis=3)
+        gate_weights = 2.5 * chosen / jnp.sum(chosen, axis=2, keepdims=True)
+        token_gate = jnp.sum(member * gate_weights[..., None], axis=2)
+        routed = jnp.sum(member, axis=2)
+        slot_rank = jnp.cumsum(routed, axis=1) - routed
         slot_ids = lax.iota(jnp.float32, capacity)
-        placement = routed.T[:, None, :] * (
-            slot_rank.T[:, None, :] == slot_ids[None, :, None]
+        placement = jnp.swapaxes(routed, 1, 2)[:, :, None, :] * (
+            jnp.swapaxes(slot_rank, 1, 2)[:, :, None, :] == slot_ids[None, None, :, None]
         ).astype(jnp.float32)
         packed = jnp.einsum(
-            "ect,tf->ecf",
+            "mect,mtf->emcf",
             placement.astype(jnp.bfloat16),
             normed,
             preferred_element_type=jnp.float32,
         ).astype(jnp.bfloat16)
+        packed = packed.reshape(expert_count, micro_count * capacity, model_width)
         send_rows = jnp.repeat(packed, 2, axis=0)
         recv_rows = lax.all_to_all(send_rows, "ep", split_axis=0, concat_axis=0, tiled=True)
         sources = recv_rows.shape[0]
@@ -75,33 +76,27 @@
         part = expert_rows(recv_rows.reshape(sources * item_count, model_width))
         part = part.reshape(sources, item_count, model_width)
         home_back = lax.all_to_all(part, "ep", split_axis=0, concat_axis=0, tiled=True)
-        combined = home_back.astype(jnp.float32).reshape(expert_count, 2, capacity, model_width)
+        combined = home_back.astype(jnp.float32).reshape(
+            expert_count, 2, micro_count, capacity, model_width
+        )
         pair_sum = combined[:, 0] + combined[:, 1]
-        weighting = placement * token_gate.T[:, None, :]
-        routed_sum = jnp.einsum("ect,ecf->tf", weighting, pair_sum, precision=lax.Precision.HIGHEST)
+        weighting = placement * jnp.swapaxes(token_gate, 1, 2)[:, :, None, :]
+        routed_sum = jnp.einsum(
+            "mect,emcf->mtf", weighting, pair_sum, precision=lax.Precision.HIGHEST
+        )
         return (rows_float + routed_sum).astype(jnp.bfloat16)
 
-    def run_tick(tick_index, loop_state):
+    route_ids = routes[0]
+
+    def run_step(step, loop_state):
         incoming, outputs = loop_state
-        micro_index = tick_index - section_index
-        is_live = (micro_index >= 0) & (micro_index < micro_count)
-        clipped = jnp.clip(micro_index, 0, micro_count - 1)
-        fresh_rows = lax.dynamic_index_in_dim(rows_in, clipped, 0, keepdims=False)
-        layer_input = jnp.where(section_index == 0, fresh_rows, incoming)
-        route_ids = lax.dynamic_index_in_dim(routes[0], clipped, 0, keepdims=False)
+        layer_input = jnp.where(section_index == 0, rows_in, incoming)
         next_rows = apply_layer(layer_input, route_ids)
-        updated = lax.dynamic_update_index_in_dim(outputs, next_rows, clipped, 0)
-        outputs = jnp.where(is_live, updated, outputs)
-        incoming = shifted(next_rows, "section", 1)
-        return (incoming, outputs)
+        outputs = jnp.where(section_index == step, next_rows, outputs)
+        return (shifted(next_rows, "section", 1), outputs)
 
-    tick_count = micro_count + section_count - 1
-    start_state = (
-        jnp.zeros((tok_rows, model_width), jnp.bfloat16),
-        jnp.zeros(rows_in.shape, jnp.bfloat16),
-    )
-    final_state = lax.fori_loop(0, tick_count, run_tick, start_state)
-    outputs = final_state[1]
+    start_state = (jnp.zeros(rows_in.shape, jnp.bfloat16), jnp.zeros(rows_in.shape, jnp.bfloat16))
+    outputs = lax.fori_loop(0, section_count, run_step, start_state)[1]
     unit_count = home_units * (2.0 - (owner_index == ep_index).astype(jnp.float32)) + own_hot
     relative = unit_count / float(micro_count * tok_rows * top_count * blocks_per_expert)
     return (outputs[None], relative.reshape(1, 1))

time: 416 us -> 513 us (1.23)
  the two profiles are of different devices: /device:TPU:0 before, /device:TPU:1 now
where the time goes in v2:
time: 513 us; the launch traced here: 512 us
  blocking collectives  194 us (38%)
  waiting for transfers between devices  190 us (37%)
  matrix products  64.8 us (13%)
  starting transfers between devices  27.7 us (5%)
  other arithmetic  16.5 us (3%)
  local copies, waits for them, and re-layouts  14.9 us (3%)
    all_to_all x4, blocking collectives, apply_layer(): lax.all_to_all(send_rows, 'ep', split_axis=0, concat_axis=0, tiled=True)  175 us
    all_to_all x4, waiting for transfers between devices, apply_layer(): lax.all_to_all(part, 'ep', split_axis=0, concat_axis=0, tiled=True)  169 us
    dot_general x4, matrix products, expert_rows(): jnp.dot(activation, down_w, preferred_element_type=jnp.float32)  34.6 us
    ppermute x4, waiting for transfers between devices, shifted(): return lax.ppermute(block, axis, route)  21.6 us
    psum x1, blocking collectives, local(): expert_total = lax.psum(expert_local, 'ep')  18.7 us
    all_to_all x4, starting transfers between devices, apply_layer(): lax.all_to_all(part, 'ep', split_axis=0, concat_axis=0, tiled=True)  14.9 us
    dot_general x4, matrix products, apply_layer(): jnp.einsum('mect,emcf->mtf', weighting, pair_sum, precision=lax.Precision...  14.9 us
    ppermute x4, starting transfers between devices, shifted(): return lax.ppermute(block, axis, route)  12.8 us
  transfers between devices with their start and end apart: 8, of which 8 were waited for; matrix products, arithmetic and copies ran while one was open for 0% of the time, Pallas kernels for 0%

profile of v2, /device:TPU:1, one launch (start us, length us, event | category | flops | bytes accessed | tf_op | source)
XLA Modules:
  0.0 512.0 jit_solution(4193816347571856883)
XLA Ops:
  1.5 18.7 %psum.7 = f32[4]{0:T(128)S(1)} all-reduce(f32[4]{0:T(128)S(1)} %convert_reduce_fusion), channel_id=1, replica_groups=mesh['section'=4,'ep'=8] {'ep'}, use_global_device_ids=true, to_apply=%region_9.10 | all-reduce | flops 4 | bytes 32 | tf_op jit(solution)/shard_map/psum | solution.py:39
  24.1 486.0 %while.17 = (s32[]{:T(128)}, bf16[4,8,7168]{2,1,0:T(8,128)(2,1)S(1)}, bf16[4,8,7168]{2,1,0:T(8,128)(2,1)S(1)}, pred[]{:T(512)}, bf16[4,8,7168]{2,1,0:T(8,128)(2,...) while((s32[]{:T(128)}, ...), condition=%wide.region_7.8_spmd.clone, body=%wide.region_0.7_spmd.clone.sunk | while | flops 2877921280 | bytes 92975272 | solution.py:99
  29.0 43.1 %all_to_all.24 = bf16[8,16,7168]{2,1,0:T(8,128)(2,1)S(1)} all-to-all(bf16[8,16,7168]{2,1,0:T(8,128)(2,1)S(1)} %bitcast.91), channel_id=1, replica_groups=mesh['section'=4,'ep'=8] {'ep'}, dimensions={0} | all-to-all | bytes 3670016 | tf_op jit(solution)/shard_map/while/body/eval_jaxpr/all_to_all | solution.py:73
  73.2 8.6 %convolution_convert_fusion.3 = bf16[128,7168]{1,0:T(8,128)(2,1)} fusion(bf16[512,7168]{1,0:T(8,128)(2,1)} %get-tuple-element.493, bf16[128,7168]{1,0:T(8,128)(2,1)S(1)} %bitcast.86, bf16[7168,512]{1,0:T(8,128)(2,1)} %get-tuple-element.492, f32[128,512]{1,0:T(8,128)S(1)} %fusion.71), kind=kOutput, calls=%fused_computation.1.clone.1 | convolution fusion | flops 1880358912 | bytes 18612224 | tf_op jit(solution)/shard_map/while/body/eval_jaxpr/dot_general | solution.py:48
  81.9 4.1 all-to-all-start.1
  86.0 40.2 %all-to-all-done.1 = bf16[8,16,7168]{2,1,0:T(8,128)(2,1)S(1)} async-done(((bf16[8,16,7168]{2,1,0:T(8,128)(2,1)}), bf16[8,16,7168]{2,1,0:T(8,128)(2,1)S(1)}, u32[]{:S(2)}, u32[]{:S(2)}) %all-to-all-start.1) | async-done | bytes 1835040 | tf_op jit(solution)/shard_map/while/body/eval_jaxpr/all_to_all | solution.py:78
  126.2 2.4 reshape.91
  128.6 2.5 fusion.72
  131.1 3.7 select_select_fusion.2
  134.8 7.1 %collective-permute-start = (bf16[4,8,7168]{2,1,0:T(8,128)(2,1)S(1)}, bf16[4,8,7168]{2,1,0:T(8,128)(2,1)S(1)}, u32[]{:S(2)}, u32[]{:S(2)}) collective-permute-start(bf16[4,8,7168]{2,1,0:T(8,128)(2,1)S(1)} %get-tuple-element.451), channel_id=1, source_target_pairs={{0,8},{8,16},{16,24},{1,9},{9,17},{17,25},{2,10},{10,18},{18,26},{... | collective-permute-start | bytes 1376264 | tf_op jit(solution)/shard_map/while/body/eval_jaxpr/ppermute | solution.py:13
  141.9 5.4 %collective-permute-done = bf16[4,8,7168]{2,1,0:T(8,128)(2,1)S(1)} collective-permute-done((bf16[4,8,7168]{2,1,0:T(8,128)(2,1)S(1)}, bf16[4,8,7168]{2,1,0:T(8,128)(2,1)S(1)}, u32[]{:S(2)}, u32[]{:S(2)}) %collective-permute-start) | collective-permute-done | bytes 458784 | tf_op jit(solution)/shard_map/while/body/eval_jaxpr/ppermute | solution.py:13
  152.2 42.3 %all_to_all.24 = bf16[8,16,7168]{2,1,0:T(8,128)(2,1)S(1)} all-to-all(bf16[8,16,7168]{2,1,0:T(8,128)(2,1)S(1)} %bitcast.91), channel_id=1, replica_groups=mesh['section'=4,'ep'=8] {'ep'}, dimensions={0} | all-to-all | bytes 3670016 | tf_op jit(solution)/shard_map/while/body/eval_jaxpr/all_to_all | solution.py:73
  195.6 8.6 %convolution_convert_fusion.3 = bf16[128,7168]{1,0:T(8,128)(2,1)} fusion(bf16[512,7168]{1,0:T(8,128)(2,1)} %get-tuple-element.493, bf16[128,7168]{1,0:T(8,128)(2,1)S(1)} %bitcast.86, bf16[7168,512]{1,0:T(8,128)(2,1)} %get-tuple-element.492, f32[128,512]{1,0:T(8,128)S(1)} %fusion.71), kind=kOutput, calls=%fused_computation.1.clone.1 | convolution fusion | flops 1880358912 | bytes 18612224 | tf_op jit(solution)/shard_map/while/body/eval_jaxpr/dot_general | solution.py:48
  204.2 3.6 all-to-all-start.1
  207.8 43.3 %all-to-all-done.1 = bf16[8,16,7168]{2,1,0:T(8,128)(2,1)S(1)} async-done(((bf16[8,16,7168]{2,1,0:T(8,128)(2,1)}), bf16[8,16,7168]{2,1,0:T(8,128)(2,1)S(1)}, u32[]{:S(2)}, u32[]{:S(2)}) %all-to-all-start.1) | async-done | bytes 1835040 | tf_op jit(solution)/shard_map/while/body/eval_jaxpr/all_to_all | solution.py:78
  253.5 2.5 fusion.72
  256.0 3.7 select_select_fusion.2
  261.7 5.4 %collective-permute-done = bf16[4,8,7168]{2,1,0:T(8,128)(2,1)S(1)} collective-permute-done((bf16[4,8,7168]{2,1,0:T(8,128)(2,1)S(1)}, bf16[4,8,7168]{2,1,0:T(8,128)(2,1)S(1)}, u32[]{:S(2)}, u32[]{:S(2)}) %collective-permute-start) | collective-permute-done | bytes 458784 | tf_op jit(solution)/shard_map/while/body/eval_jaxpr/ppermute | solution.py:13
  271.9 44.4 %all_to_all.24 = bf16[8,16,7168]{2,1,0:T(8,128)(2,1)S(1)} all-to-all(bf16[8,16,7168]{2,1,0:T(8,128)(2,1)S(1)} %bitcast.91), channel_id=1, replica_groups=mesh['section'=4,'ep'=8] {'ep'}, dimensions={0} | all-to-all | bytes 3670016 | tf_op jit(solution)/shard_map/while/body/eval_jaxpr/all_to_all | solution.py:73
  317.4 8.6 %convolution_convert_fusion.3 = bf16[128,7168]{1,0:T(8,128)(2,1)} fusion(bf16[512,7168]{1,0:T(8,128)(2,1)} %get-tuple-element.493, bf16[128,7168]{1,0:T(8,128)(2,1)S(1)} %bitcast.86, bf16[7168,512]{1,0:T(8,128)(2,1)} %get-tuple-element.492, f32[128,512]{1,0:T(8,128)S(1)} %fusion.71), kind=kOutput, calls=%fused_computation.1.clone.1 | convolution fusion | flops 1880358912 | bytes 18612224 | tf_op jit(solution)/shard_map/while/body/eval_jaxpr/dot_general | solution.py:48
  326.1 3.6 all-to-all-start.1
  329.7 42.6 %all-to-all-done.1 = bf16[8,16,7168]{2,1,0:T(8,128)(2,1)S(1)} async-done(((bf16[8,16,7168]{2,1,0:T(8,128)(2,1)}), bf16[8,16,7168]{2,1,0:T(8,128)(2,1)S(1)}, u32[]{:S(2)}, u32[]{:S(2)}) %all-to-all-start.1) | async-done | bytes 1835040 | tf_op jit(solution)/shard_map/while/body/eval_jaxpr/all_to_all | solution.py:78
  374.7 2.5 fusion.72
  377.2 3.7 select_select_fusion.2
  382.8 5.4 %collective-permute-done = bf16[4,8,7168]{2,1,0:T(8,128)(2,1)S(1)} collective-permute-done((bf16[4,8,7168]{2,1,0:T(8,128)(2,1)S(1)}, bf16[4,8,7168]{2,1,0:T(8,128)(2,1)S(1)}, u32[]{:S(2)}, u32[]{:S(2)}) %collective-permute-start) | collective-permute-done | bytes 458784 | tf_op jit(solution)/shard_map/while/body/eval_jaxpr/ppermute | solution.py:13
  393.1 45.1 %all_to_all.24 = bf16[8,16,7168]{2,1,0:T(8,128)(2,1)S(1)} all-to-all(bf16[8,16,7168]{2,1,0:T(8,128)(2,1)S(1)} %bitcast.91), channel_id=1, replica_groups=mesh['section'=4,'ep'=8] {'ep'}, dimensions={0} | all-to-all | bytes 3670016 | tf_op jit(solution)/shard_map/while/body/eval_jaxpr/all_to_all | solution.py:73
  439.3 8.6 %convolution_convert_fusion.3 = bf16[128,7168]{1,0:T(8,128)(2,1)} fusion(bf16[512,7168]{1,0:T(8,128)(2,1)} %get-tuple-element.493, bf16[128,7168]{1,0:T(8,128)(2,1)S(1)} %bitcast.86, bf16[7168,512]{1,0:T(8,128)(2,1)} %get-tuple-element.492, f32[128,512]{1,0:T(8,128)S(1)} %fusion.71), kind=kOutput, calls=%fused_computation.1.clone.1 | convolution fusion | flops 1880358912 | bytes 18612224 | tf_op jit(solution)/shard_map/while/body/eval_jaxpr/dot_general | solution.py:48
  447.9 3.6 all-to-all-start.1
  451.5 42.6 %all-to-all-done.1 = bf16[8,16,7168]{2,1,0:T(8,128)(2,1)S(1)} async-done(((bf16[8,16,7168]{2,1,0:T(8,128)(2,1)}), bf16[8,16,7168]{2,1,0:T(8,128)(2,1)S(1)}, u32[]{:S(2)}, u32[]{:S(2)}) %all-to-all-start.1) | async-done | bytes 1835040 | tf_op jit(solution)/shard_map/while/body/eval_jaxpr/all_to_all | solution.py:78
  496.5 2.5 fusion.72
  499.1 3.7 select_select_fusion.2
  504.7 5.4 %collective-permute-done = bf16[4,8,7168]{2,1,0:T(8,128)(2,1)S(1)} collective-permute-done((bf16[4,8,7168]{2,1,0:T(8,128)(2,1)S(1)}, bf16[4,8,7168]{2,1,0:T(8,128)(2,1)S(1)}, u32[]{:S(2)}, u32[]{:S(2)}) %collective-permute-start) | collective-permute-done | bytes 458784 | tf_op jit(solution)/shard_map/while/body/eval_jaxpr/ppermute | solution.py:13
  (90 shorter events, 40.0 us)
Async XLA Ops:
  24.1 3.2 copy-start.2
  28.5 43.7 %copy-start = (bf16[7168,512]{1,0:T(8,128)(2,1)S(1)}, bf16[7168,512]{1,0:T(8,128)(2,1)}, u32[]{:S(2)}) copy-start(bf16[7168,512]{1,0:T(8,128)(2,1)} %get-tuple-element.491) | copy-start | bytes 22020100 | tf_op jit(solution)/shard_map/while
  81.9 44.3 %all-to-all-start.1 = ((bf16[8,16,7168]{2,1,0:T(8,128)(2,1)}), bf16[8,16,7168]{2,1,0:T(8,128)(2,1)S(1)}, u32[]{:S(2)}, u32[]{:S(2)}) async-start(bf16[8,16,7168]{2,1,0:T(8,128)(2,1)} %bitcast.88), calls=%async_computation.1 | async-start | bytes 3670016 | tf_op jit(solution)/shard_map/while/body/eval_jaxpr/all_to_all | solution.py:78
  134.8 12.5 %collective-permute-start = (bf16[4,8,7168]{2,1,0:T(8,128)(2,1)S(1)}, bf16[4,8,7168]{2,1,0:T(8,128)(2,1)S(1)}, u32[]{:S(2)}, u32[]{:S(2)}) collective-permute-start(bf16[4,8,7168]{2,1,0:T(8,128)(2,1)S(1)} %get-tuple-element.451), channel_id=1, source_target_pairs={{0,8},{8,16},{16,24},{1,9},{9,17},{17,25},{2,10},{10,18},{18,26},{... | collective-permute-start | bytes 1376264 | tf_op jit(solution)/shard_map/while/body/eval_jaxpr/ppermute | solution.py:13
  147.3 3.2 copy-start.2
  151.6 42.8 %copy-start = (bf16[7168,512]{1,0:T(8,128)(2,1)S(1)}, bf16[7168,512]{1,0:T(8,128)(2,1)}, u32[]{:S(2)}) copy-start(bf16[7168,512]{1,0:T(8,128)(2,1)} %get-tuple-element.491) | copy-start | bytes 22020100 | tf_op jit(solution)/shard_map/while
  204.2 46.9 %all-to-all-start.1 = ((bf16[8,16,7168]{2,1,0:T(8,128)(2,1)}), bf16[8,16,7168]{2,1,0:T(8,128)(2,1)S(1)}, u32[]{:S(2)}, u32[]{:S(2)}) async-start(bf16[8,16,7168]{2,1,0:T(8,128)(2,1)} %bitcast.88), calls=%async_computation.1 | async-start | bytes 3670016 | tf_op jit(solution)/shard_map/while/body/eval_jaxpr/all_to_all | solution.py:78
  259.8 7.3 %collective-permute-start = (bf16[4,8,7168]{2,1,0:T(8,128)(2,1)S(1)}, bf16[4,8,7168]{2,1,0:T(8,128)(2,1)S(1)}, u32[]{:S(2)}, u32[]{:S(2)}) collective-permute-start(bf16[4,8,7168]{2,1,0:T(8,128)(2,1)S(1)} %get-tuple-element.451), channel_id=1, source_target_pairs={{0,8},{8,16},{16,24},{1,9},{9,17},{17,25},{2,10},{10,18},{18,26},{... | collective-permute-start | bytes 1376264 | tf_op jit(solution)/shard_map/while/body/eval_jaxpr/ppermute | solution.py:13
  267.1 3.2 copy-start.2
  271.4 44.9 %copy-start = (bf16[7168,512]{1,0:T(8,128)(2,1)S(1)}, bf16[7168,512]{1,0:T(8,128)(2,1)}, u32[]{:S(2)}) copy-start(bf16[7168,512]{1,0:T(8,128)(2,1)} %get-tuple-element.491) | copy-start | bytes 22020100 | tf_op jit(solution)/shard_map/while
  326.1 46.2 %all-to-all-start.1 = ((bf16[8,16,7168]{2,1,0:T(8,128)(2,1)}), bf16[8,16,7168]{2,1,0:T(8,128)(2,1)S(1)}, u32[]{:S(2)}, u32[]{:S(2)}) async-start(bf16[8,16,7168]{2,1,0:T(8,128)(2,1)} %bitcast.88), calls=%async_computation.1 | async-start | bytes 3670016 | tf_op jit(solution)/shard_map/while/body/eval_jaxpr/all_to_all | solution.py:78
  380.9 7.3 %collective-permute-start = (bf16[4,8,7168]{2,1,0:T(8,128)(2,1)S(1)}, bf16[4,8,7168]{2,1,0:T(8,128)(2,1)S(1)}, u32[]{:S(2)}, u32[]{:S(2)}) collective-permute-start(bf16[4,8,7168]{2,1,0:T(8,128)(2,1)S(1)} %get-tuple-element.451), channel_id=1, source_target_pairs={{0,8},{8,16},{16,24},{1,9},{9,17},{17,25},{2,10},{10,18},{18,26},{... | collective-permute-start | bytes 1376264 | tf_op jit(solution)/shard_map/while/body/eval_jaxpr/ppermute | solution.py:13
  388.2 3.2 copy-start.2
  392.6 45.6 %copy-start = (bf16[7168,512]{1,0:T(8,128)(2,1)S(1)}, bf16[7168,512]{1,0:T(8,128)(2,1)}, u32[]{:S(2)}) copy-start(bf16[7168,512]{1,0:T(8,128)(2,1)} %get-tuple-element.491) | copy-start | bytes 22020100 | tf_op jit(solution)/shard_map/while
  447.9 46.2 %all-to-all-start.1 = ((bf16[8,16,7168]{2,1,0:T(8,128)(2,1)}), bf16[8,16,7168]{2,1,0:T(8,128)(2,1)S(1)}, u32[]{:S(2)}, u32[]{:S(2)}) async-start(bf16[8,16,7168]{2,1,0:T(8,128)(2,1)} %bitcast.88), calls=%async_computation.1 | async-start | bytes 3670016 | tf_op jit(solution)/shard_map/while/body/eval_jaxpr/all_to_all | solution.py:78
  502.8 7.3 %collective-permute-start = (bf16[4,8,7168]{2,1,0:T(8,128)(2,1)S(1)}, bf16[4,8,7168]{2,1,0:T(8,128)(2,1)S(1)}, u32[]{:S(2)}, u32[]{:S(2)}) collective-permute-start(bf16[4,8,7168]{2,1,0:T(8,128)(2,1)S(1)} %get-tuple-element.451), channel_id=1, source_target_pairs={{0,8},{8,16},{16,24},{1,9},{9,17},{17,25},{2,10},{10,18},{18,26},{... | collective-permute-start | bytes 1376264 | tf_op jit(solution)/shard_map/while/body/eval_jaxpr/ppermute | solution.py:13
  510.1 0.8 copy-start.1

commit v3 on v2

--- a/solution.py
+++ b/solution.py
@@ -91,7 +91,12 @@
     def run_step(step, loop_state):
         incoming, outputs = loop_state
         layer_input = jnp.where(section_index == 0, rows_in, incoming)
-        next_rows = apply_layer(layer_input, route_ids)
+        next_rows = lax.cond(
+            section_index == step,
+            lambda rows: apply_layer(rows, route_ids),
+            lambda rows: rows,
+            layer_input,
+        )
         outputs = jnp.where(section_index == step, next_rows, outputs)
         return (shifted(next_rows, "section", 1), outputs)
 

time: 513 us -> 364 us (0.71)
  the two profiles are of different devices: /device:TPU:1 before, /device:TPU:5 now
where the time goes in v3:
time: 364 us; the launch traced here: 363 us
  waiting for transfers between devices  254 us (70%)
  blocking collectives  71.2 us (20%)
  matrix products  16.9 us (5%)
  other arithmetic  6.63 us (2%)
  starting transfers between devices  5.17 us (1%)
  local copies, waits for them, and re-layouts  4.85 us (1%)
  between operations  3.79 us (1%)
    ppermute x4, waiting for transfers between devices, shifted(): return lax.ppermute(block, axis, route)  254 us
    all_to_all x1, blocking collectives, apply_layer(): lax.all_to_all(part, 'ep', split_axis=0, concat_axis=0, tiled=True)  26.7 us
    all_to_all x1, blocking collectives, apply_layer(): lax.all_to_all(send_rows, 'ep', split_axis=0, concat_axis=0, tiled=True)  26.6 us
    psum x1, blocking collectives, local(): expert_total = lax.psum(expert_local, 'ep')  17.9 us
    dot_general x1, matrix products, expert_rows(): jnp.dot(activation, down_w, preferred_element_type=jnp.float32)  8.63 us
  transfers between devices with their start and end apart: 4, of which 4 were waited for; matrix products, arithmetic and copies ran while one was open for 0% of the time, Pallas kernels for 0%

profile of v3, /device:TPU:5, one launch (start us, length us, event | category | flops | bytes accessed | tf_op | source)
XLA Modules:
  0.0 362.9 jit_solution(1931823930785364750)
XLA Ops:
  0.6 0.8 convert_reduce_fusion
  1.5 17.9 %psum.7 = f32[4]{0:T(128)S(1)} all-reduce(f32[4]{0:T(128)S(1)} %convert_reduce_fusion), channel_id=1, replica_groups=mesh['section'=4,'ep'=8] {'ep'}, use_global_device_ids=true, to_apply=%region_11.12 | all-reduce | flops 4 | bytes 32 | tf_op jit(solution)/shard_map/psum | solution.py:39
  19.3 0.6 fusion.33
  21.3 0.6 fusion.34
  22.6 0.7 copy.30
  23.3 337.7 %while.17 = (s32[]{:T(128)}, bf16[4,8,7168]{2,1,0:T(8,128)(2,1)S(1)}, bf16[4,8,7168]{2,1,0:T(8,128)(2,1)S(1)}, s32[]{:T(128)}, pred[]{:T(512)}, /*index=5*/bf16[...) while((s32[]{:T(128)}, ...), condition=%wide.region_9.10_spmd.clone, body=%wide.region_0.9_spmd.clone.sunk | while | flops 2877921280 | bytes 91943128 | solution.py:104
  23.4 1.3 collective-permute-start
  24.7 0.2 select_select_fusion.2
  24.9 6.2 %collective-permute-done = bf16[4,8,7168]{2,1,0:T(8,128)(2,1)S(1)} collective-permute-done((bf16[4,8,7168]{2,1,0:T(8,128)(2,1)S(1)}, bf16[4,8,7168]{2,1,0:T(8,128)(2,1)S(1)}, u32[]{:S(2)}, u32[]{:S(2)}) %collective-permute-start) | collective-permute-done | bytes 458784 | tf_op jit(solution)/shard_map/while/body/eval_jaxpr/ppermute | solution.py:13
  31.1 1.3 collective-permute-start
  32.4 0.2 select_select_fusion.2
  32.6 8.3 %collective-permute-done = bf16[4,8,7168]{2,1,0:T(8,128)(2,1)S(1)} collective-permute-done((bf16[4,8,7168]{2,1,0:T(8,128)(2,1)S(1)}, bf16[4,8,7168]{2,1,0:T(8,128)(2,1)S(1)}, u32[]{:S(2)}, u32[]{:S(2)}) %collective-permute-start) | collective-permute-done | bytes 458784 | tf_op jit(solution)/shard_map/while/body/eval_jaxpr/ppermute | solution.py:13
  41.0 1.3 collective-permute-start
  42.5 237.4 %collective-permute-done = bf16[4,8,7168]{2,1,0:T(8,128)(2,1)S(1)} collective-permute-done((bf16[4,8,7168]{2,1,0:T(8,128)(2,1)S(1)}, bf16[4,8,7168]{2,1,0:T(8,128)(2,1)S(1)}, u32[]{:S(2)}, u32[]{:S(2)}) %collective-permute-start) | collective-permute-done | bytes 458784 | tf_op jit(solution)/shard_map/while/body/eval_jaxpr/ppermute | solution.py:13
  279.9 77.3 %conditional.3 = (bf16[4,8,7168]{2,1,0:T(8,128)(2,1)S(1)}) conditional(s32[]{:T(128)} %convert_element_type.78, bf16[4,8,7168]{2,1,0:T(8,128)(2,1)S(1)} %broadcast_select_fusion.2, (bf16[4,8,7168]{2,1,0:T(8,128)(2,1)S(1)}, s32[1,4,8,2]{2,1,3,0:T(4,128)S(1)}, s32[4]{0:T(128)S(1)}, f32[1,7168]{1,0:T(1,128)}, bf16[7168,4]{0,1:T(4,128)(2,1)}, ...), branch_computations={%region_1.1_spmd, %region_2.8_spmd} | conditional | flops 2877233152 | bytes 87355336 | solution.py:94
  280.0 0.2 fusion.11
  280.2 2.0 fusion.10
  282.4 0.7 reduce_window_sum.11
  283.2 1.4 fusion.2
  284.6 0.5 copy.27
  285.1 0.3 copy.28
  285.4 0.2 broadcast_in_dim.6
  285.6 26.6 %all_to_all.8 = bf16[8,16,7168]{2,1,0:T(8,128)(2,1)S(1)} all-to-all(bf16[8,16,7168]{2,1,0:T(8,128)(2,1)S(1)} %bitcast.53), channel_id=1, replica_groups=mesh['section'=4,'ep'=8] {'ep'}, dimensions={0} | all-to-all | bytes 3670016 | tf_op jit(solution)/shard_map/while/body/eval_jaxpr/cond/branch_1_fun/all_to_all | solution.py:73
  312.2 1.1 fusion.35
  313.3 8.6 %convolution_convert_fusion = bf16[128,7168]{1,0:T(8,128)(2,1)} fusion(bf16[512,7168]{1,0:T(8,128)(2,1)} %get-tuple-element.269, bf16[128,7168]{1,0:T(8,128)(2,1)S(1)} %bitcast.48, bf16[7168,512]{1,0:T(8,128)(2,1)} %get-tuple-element.268, f32[128,512]{1,0:T(8,128)S(1)} %fusion.35), kind=kOutput, calls=%fused_computation.1 | convolution fusion | flops 1880358912 | bytes 18612224 | tf_op jit(solution)/shard_map/while/body/eval_jaxpr/cond/branch_1_fun/dot_general | solution.py:48
  322.0 26.7 %all_to_all.9 = bf16[8,16,7168]{2,1,0:T(8,128)(2,1)S(1)} all-to-all(bf16[8,16,7168]{2,1,0:T(8,128)(2,1)} %bitcast.50), channel_id=1, replica_groups=mesh['section'=4,'ep'=8] {'ep'}, dimensions={0} | all-to-all | bytes 3670016 | tf_op jit(solution)/shard_map/while/body/eval_jaxpr/cond/branch_1_fun/all_to_all | solution.py:78
  348.7 2.4 reshape.49
  351.1 2.5 fusion.5
  353.6 3.7 %fusion.4 = bf16[4,8,7168]{2,1,0:T(8,128)(2,1)S(1)} fusion(f32[4,4,4,7168]{3,2,1,0:T(4,128)S(1)} %fusion.5, bf16[4,8,7168]{2,1,0:T(8,128)(2,1)S(1)} %get-tuple-element.262, f32[4,4,8]{2,1,0:T(4,128)S(1)} %bitcast.58, f32[4,4,8]{2,1,0:T(4,128)S(1)} %bitcast.57, f32[4,4,8]{2,1,0:T(4,128)S(1)} %bitcast_subtract_fusion), kind=kOutput, calls=%fused_computation.6 | convolution fusion | flops 44729856 | bytes 2754048 | tf_op jit(solution)/shard_map/while/body/eval_jaxpr/cond/branch_1_fun/mect,emcf->mtf/dot_general | solution.py:84
  357.3 1.3 collective-permute-start
  358.8 2.2 collective-permute-done
  361.0 0.8 copy-done.1
  (25 shorter events, 0.9 us)
Async XLA Ops:
  23.4 7.6 %collective-permute-start = (bf16[4,8,7168]{2,1,0:T(8,128)(2,1)S(1)}, bf16[4,8,7168]{2,1,0:T(8,128)(2,1)S(1)}, u32[]{:S(2)}, u32[]{:S(2)}) collective-permute-start(bf16[4,8,7168]{2,1,0:T(8,128)(2,1)S(1)} %get-tuple-element.508), channel_id=1, source_target_pairs={{0,8},{8,16},{16,24},{1,9},{9,17},{17,25},{2,10},{10,18},{18,26},{... | collective-permute-start | bytes 1376264 | tf_op jit(solution)/shard_map/while/body/eval_jaxpr/ppermute | solution.py:13
  31.1 9.8 %collective-permute-start = (bf16[4,8,7168]{2,1,0:T(8,128)(2,1)S(1)}, bf16[4,8,7168]{2,1,0:T(8,128)(2,1)S(1)}, u32[]{:S(2)}, u32[]{:S(2)}) collective-permute-start(bf16[4,8,7168]{2,1,0:T(8,128)(2,1)S(1)} %get-tuple-element.508), channel_id=1, source_target_pairs={{0,8},{8,16},{16,24},{1,9},{9,17},{17,25},{2,10},{10,18},{18,26},{... | collective-permute-start | bytes 1376264 | tf_op jit(solution)/shard_map/while/body/eval_jaxpr/ppermute | solution.py:13
  41.0 238.9 %collective-permute-start = (bf16[4,8,7168]{2,1,0:T(8,128)(2,1)S(1)}, bf16[4,8,7168]{2,1,0:T(8,128)(2,1)S(1)}, u32[]{:S(2)}, u32[]{:S(2)}) collective-permute-start(bf16[4,8,7168]{2,1,0:T(8,128)(2,1)S(1)} %get-tuple-element.508), channel_id=1, source_target_pairs={{0,8},{8,16},{16,24},{1,9},{9,17},{17,25},{2,10},{10,18},{18,26},{... | collective-permute-start | bytes 1376264 | tf_op jit(solution)/shard_map/while/body/eval_jaxpr/ppermute | solution.py:13
  285.1 27.1 %copy-start = (bf16[7168,512]{1,0:T(8,128)(2,1)S(1)}, bf16[7168,512]{1,0:T(8,128)(2,1)}, u32[]{:S(2)}) copy-start(bf16[7168,512]{1,0:T(8,128)(2,1)} %get-tuple-element.267) | copy-start | bytes 22020100 | tf_op jit(solution)/shard_map/while/body/eval_jaxpr/cond
  357.3 3.7 %collective-permute-start = (bf16[4,8,7168]{2,1,0:T(8,128)(2,1)S(1)}, bf16[4,8,7168]{2,1,0:T(8,128)(2,1)S(1)}, u32[]{:S(2)}, u32[]{:S(2)}) collective-permute-start(bf16[4,8,7168]{2,1,0:T(8,128)(2,1)S(1)} %get-tuple-element.508), channel_id=1, source_target_pairs={{0,8},{8,16},{16,24},{1,9},{9,17},{17,25},{2,10},{10,18},{18,26},{... | collective-permute-start | bytes 1376264 | tf_op jit(solution)/shard_map/while/body/eval_jaxpr/ppermute | solution.py:13
  361.0 0.8 copy-start.1

commit v4 on v3

--- a/solution.py
+++ b/solution.py
@@ -36,9 +36,6 @@
 
     route_member = (routes[0][..., None] == expert_ids).astype(jnp.float32)
     expert_local = jnp.sum(route_member, axis=(0, 1, 2))
-    expert_total = lax.psum(expert_local, "ep")
-    own_expert = ep_index // 2
-    home_units = jnp.sum(jnp.where(expert_ids == own_expert, expert_total, 0.0))
     own_hot = jnp.sum(jnp.where(expert_ids == hot_expert, expert_local, 0.0))
 
     def expert_rows(flat_rows):
@@ -68,11 +65,16 @@
             normed,
             preferred_element_type=jnp.float32,
         ).astype(jnp.bfloat16)
-        packed = packed.reshape(expert_count, micro_count * capacity, model_width)
-        send_rows = jnp.repeat(packed, 2, axis=0)
-        recv_rows = lax.all_to_all(send_rows, "ep", split_axis=0, concat_axis=0, tiled=True)
+        item_count = micro_count * capacity
+        packed = packed.reshape(expert_count, item_count, model_width)
+        count_row = jnp.broadcast_to(
+            jnp.sum(routed, axis=(0, 1))[:, None, None], (expert_count, 1, model_width)
+        ).astype(jnp.bfloat16)
+        send_rows = jnp.repeat(jnp.concatenate([packed, count_row], axis=1), 2, axis=0)
+        recv_all = lax.all_to_all(send_rows, "ep", split_axis=0, concat_axis=0, tiled=True)
+        recv_rows = recv_all[:, :item_count]
+        filled = jnp.sum(recv_all[:, item_count, 0].astype(jnp.float32))
         sources = recv_rows.shape[0]
-        item_count = recv_rows.shape[1]
         part = expert_rows(recv_rows.reshape(sources * item_count, model_width))
         part = part.reshape(sources, item_count, model_width)
         home_back = lax.all_to_all(part, "ep", split_axis=0, concat_axis=0, tiled=True)
@@ -84,24 +86,28 @@
         routed_sum = jnp.einsum(
             "mect,emcf->mtf", weighting, pair_sum, precision=lax.Precision.HIGHEST
         )
-        return (rows_float + routed_sum).astype(jnp.bfloat16)
+        return ((rows_float + routed_sum).astype(jnp.bfloat16), filled)
 
     route_ids = routes[0]
 
     def run_step(step, loop_state):
-        incoming, outputs = loop_state
+        incoming, outputs, home_units = loop_state
         layer_input = jnp.where(section_index == 0, rows_in, incoming)
-        next_rows = lax.cond(
+        next_rows, filled = lax.cond(
             section_index == step,
             lambda rows: apply_layer(rows, route_ids),
-            lambda rows: rows,
+            lambda rows: (rows, jnp.float32(0.0)),
             layer_input,
         )
         outputs = jnp.where(section_index == step, next_rows, outputs)
-        return (shifted(next_rows, "section", 1), outputs)
+        return (shifted(next_rows, "section", 1), outputs, home_units + filled)
 
-    start_state = (jnp.zeros(rows_in.shape, jnp.bfloat16), jnp.zeros(rows_in.shape, jnp.bfloat16))
-    outputs = lax.fori_loop(0, section_count, run_step, start_state)[1]
+    start_state = (
+        jnp.zeros(rows_in.shape, jnp.bfloat16),
+        jnp.zeros(rows_in.shape, jnp.bfloat16),
+        jnp.float32(0.0),
+    )
+    _, outputs, home_units = lax.fori_loop(0, section_count, run_step, start_state)
     unit_count = home_units * (2.0 - (owner_index == ep_index).astype(jnp.float32)) + own_hot
     relative = unit_count / float(micro_count * tok_rows * top_count * blocks_per_expert)
     return (outputs[None], relative.reshape(1, 1))

time: 364 us -> 397 us (1.091)
  waiting for transfers between devices: 254 us -> 316 us
  blocking collectives: 71.2 us -> 36.4 us
    ppermute x4, waiting for transfers between devices: 254 us -> 294 us  [shifted(): return lax.ppermute(block, axis, route)]
    all_to_all x1 -> x0, blocking collectives: 26.7 us -> none  [apply_layer(): lax.all_to_all(part, 'ep', split_axis=0, concat_axis=0, tiled=True)]
    all_to_all x0 -> x1, waiting for transfers between devices: none -> 21.8 us  [apply_layer(): lax.all_to_all(part, 'ep', split_axis=0, concat_axis=0, tiled=True)]
    psum x1 -> x0, blocking collectives: 17.9 us -> none  [local(): expert_total = lax.psum(expert_local, 'ep')]
    all_to_all x1, blocking collectives: 26.6 us -> 36.4 us  [apply_layer(): lax.all_to_all(send_rows, 'ep', split_axis=0, concat_axis=0, tiled=True)]
  transfers between devices with their start and end apart: 4 -> 5, of which waited for: 4 -> 5; matrix products, arithmetic and copies ran while one was open for 0% -> 1% of each run, Pallas kernels for 0% -> 0%
where the time goes in v4:
time: 397 us; the launch traced here: 396 us
  waiting for transfers between devices  316 us (80%)
  blocking collectives  36.4 us (9%)
  matrix products  16.8 us (4%)
  starting transfers between devices  8.76 us (2%)
  other arithmetic  7.52 us (2%)
  local copies, waits for them, and re-layouts  6.76 us (2%)
    ppermute x4, waiting for transfers between devices, shifted(): return lax.ppermute(block, axis, route)  294 us
    all_to_all x1, blocking collectives, apply_layer(): lax.all_to_all(send_rows, 'ep', split_axis=0, concat_axis=0, tiled=True)  36.4 us
    all_to_all x1, waiting for transfers between devices, apply_layer(): lax.all_to_all(part, 'ep', split_axis=0, concat_axis=0, tiled=True)  21.8 us
    dot_general x1, matrix products, expert_rows(): jnp.dot(activation, down_w, preferred_element_type=jnp.float32)  8.6 us
  transfers between devices with their start and end apart: 5, of which 5 were waited for; matrix products, arithmetic and copies ran while one was open for 1% of the time, Pallas kernels for 0%

profile of v4, /device:TPU:5, one launch (start us, length us, event | category | flops | bytes accessed | tf_op | source)
XLA Modules:
  0.0 396.4 jit_solution(12067592058736210471)
XLA Ops:
  1.3 0.8 convert_reduce_fusion.3
  2.1 0.7 fusion.32
  2.8 0.7 copy.48
  3.5 391.0 %while.19 = (s32[]{:T(128)}, bf16[4,8,7168]{2,1,0:T(8,128)(2,1)S(1)}, bf16[4,8,7168]{2,1,0:T(8,128)(2,1)S(1)}, f32[]{:T(128)}, s32[]{:T(128)}, /*index=5*/pred[]...) while((s32[]{:T(128)}, ...), condition=%wide.region_11.12_spmd.clone, body=%wide.region_0.11_spmd.clone.sunk | while | flops 2878408960 | bytes 100430240 | solution.py:110
  3.6 1.3 collective-permute-start
  5.1 2.4 collective-permute-done
  7.6 1.3 collective-permute-start
  9.1 8.3 %collective-permute-done = bf16[4,8,7168]{2,1,0:T(8,128)(2,1)S(1)} collective-permute-done((bf16[4,8,7168]{2,1,0:T(8,128)(2,1)S(1)}, bf16[4,8,7168]{2,1,0:T(8,128)(2,1)S(1)}, u32[]{:S(2)}, u32[]{:S(2)}) %collective-permute-start) | collective-permute-done | bytes 458784 | tf_op jit(solution)/shard_map/while/body/eval_jaxpr/ppermute | solution.py:13
  17.5 1.3 collective-permute-start
  19.0 281.2 %collective-permute-done = bf16[4,8,7168]{2,1,0:T(8,128)(2,1)S(1)} collective-permute-done((bf16[4,8,7168]{2,1,0:T(8,128)(2,1)S(1)}, bf16[4,8,7168]{2,1,0:T(8,128)(2,1)S(1)}, u32[]{:S(2)}, u32[]{:S(2)}) %collective-permute-start) | collective-permute-done | bytes 458784 | tf_op jit(solution)/shard_map/while/body/eval_jaxpr/ppermute | solution.py:13
  300.3 90.5 %conditional.3 = (bf16[4,8,7168]{2,1,0:T(8,128)(2,1)S(1)}, f32[]{:T(128)}) conditional(s32[]{:T(128)} %convert_element_type.91, bf16[4,8,7168]{2,1,0:T(8,128)(2,1)S(1)} %broadcast_select_fusion.2, (bf16[4,8,7168]{2,1,0:T(8,128)(2,1)S(1)}, s32[1,4,8,2]{2,1,3,0:T(4,128)S(1)}, s32[4]{0:T(128)S(1)}, f32[1,7168]{1,0:T(1,128)}, bf16[7168,4]{0,1:T(4,128)(2,1)}, ...), branch_computations={%region_1.1_spmd, %region_2.10_spmd} | conditional | flops 2877720832 | bytes 95842432 | solution.py:96
  300.3 0.2 fusion.11
  300.5 2.0 fusion.10
  302.9 0.7 reduce_window_sum.11
  303.6 1.4 fusion.2
  305.0 0.5 copy.44
  305.6 0.7 pad_maximum_fusion
  306.3 0.3 copy.55
  306.6 0.3 broadcast_in_dim.5.clone
  306.9 36.4 %all_to_all.8 = bf16[8,17,7168]{2,1,0:T(8,128)(2,1)S(1)} all-to-all(bf16[8,17,7168]{2,1,0:T(8,128)(2,1)S(1)} %bitcast.52), channel_id=1, replica_groups=mesh['section'=4,'ep'=8] {'ep'}, dimensions={0} | all-to-all | bytes 3899392 | tf_op jit(solution)/shard_map/while/body/eval_jaxpr/cond/branch_1_fun/all_to_all | solution.py:74
  343.5 1.4 copy-done
  344.9 1.1 fusion.33
  346.1 8.6 %convolution_convert_fusion = bf16[128,7168]{1,0:T(8,128)(2,1)} fusion(bf16[512,7168]{1,0:T(8,128)(2,1)} %get-tuple-element.279, bf16[128,7168]{1,0:T(8,128)(2,1)S(1)} %bitcast.48, bf16[7168,512]{1,0:T(8,128)(2,1)} %get-tuple-element.278, f32[128,512]{1,0:T(8,128)S(1)} %fusion.33), kind=kOutput, calls=%fused_computation.1 | convolution fusion | flops 1880358912 | bytes 18612224 | tf_op jit(solution)/shard_map/while/body/eval_jaxpr/cond/branch_1_fun/dot_general | solution.py:45
  354.7 3.6 all-to-all-start.1
  358.3 0.7 slice.15
  359.1 0.7 convert_reduce_fusion.2
  359.8 21.8 %all-to-all-done.1 = bf16[8,16,7168]{2,1,0:T(8,128)(2,1)S(1)} async-done(((bf16[8,16,7168]{2,1,0:T(8,128)(2,1)}), bf16[8,16,7168]{2,1,0:T(8,128)(2,1)S(1)}, u32[]{:S(2)}, u32[]{:S(2)}) %all-to-all-start.1) | async-done | bytes 1835040 | tf_op jit(solution)/shard_map/while/body/eval_jaxpr/cond/branch_1_fun/all_to_all | solution.py:80
  381.6 2.4 reshape.57
  384.0 2.5 fusion.5
  386.5 3.7 fusion.4
  390.8 1.3 collective-permute-start
  392.3 2.2 collective-permute-done
  (35 shorter events, 1.8 us)
Async XLA Ops:
  3.6 3.9 collective-permute-start
  7.6 9.8 %collective-permute-start = (bf16[4,8,7168]{2,1,0:T(8,128)(2,1)S(1)}, bf16[4,8,7168]{2,1,0:T(8,128)(2,1)S(1)}, u32[]{:S(2)}, u32[]{:S(2)}) collective-permute-start(bf16[4,8,7168]{2,1,0:T(8,128)(2,1)S(1)} %get-tuple-element.526), channel_id=1, source_target_pairs={{0,8},{8,16},{16,24},{1,9},{9,17},{17,25},{2,10},{10,18},{18,26},{... | collective-permute-start | bytes 1376264 | tf_op jit(solution)/shard_map/while/body/eval_jaxpr/ppermute | solution.py:13
  17.5 282.7 %collective-permute-start = (bf16[4,8,7168]{2,1,0:T(8,128)(2,1)S(1)}, bf16[4,8,7168]{2,1,0:T(8,128)(2,1)S(1)}, u32[]{:S(2)}, u32[]{:S(2)}) collective-permute-start(bf16[4,8,7168]{2,1,0:T(8,128)(2,1)S(1)} %get-tuple-element.526), channel_id=1, source_target_pairs={{0,8},{8,16},{16,24},{1,9},{9,17},{17,25},{2,10},{10,18},{18,26},{... | collective-permute-start | bytes 1376264 | tf_op jit(solution)/shard_map/while/body/eval_jaxpr/ppermute | solution.py:13
  306.6 38.3 %slice-start = ((s8[7340032]{0:T(1024)(128)(4,1)}), s8[3145728]{0:T(1024)(128)(4,1)S(1)}, s32[]{:S(2)}) async-start(s8[7340032]{0:T(1024)(128)(4,1)} %bitcast.50), calls=%async_computation.2 | async-start | bytes 6291456 | tf_op jit(solution)/shard_map/while/body/eval_jaxpr/cond
  306.9 38.0 %slice-start.1 = ((s8[7340032]{0:T(1024)(128)(4,1)}), s8[4194304]{0:T(1024)(128)(4,1)S(1)}, s32[]{:S(2)}) async-start(s8[7340032]{0:T(1024)(128)(4,1)} %bitcast.50), calls=%async_computation.3 | async-start | bytes 8388608 | tf_op jit(solution)/shard_map/while/body/eval_jaxpr/cond
  343.4 1.6 copy-start
  354.7 26.9 %all-to-all-start.1 = ((bf16[8,16,7168]{2,1,0:T(8,128)(2,1)}), bf16[8,16,7168]{2,1,0:T(8,128)(2,1)S(1)}, u32[]{:S(2)}, u32[]{:S(2)}) async-start(bf16[8,16,7168]{2,1,0:T(8,128)(2,1)} %bitcast.53), calls=%async_computation.1 | async-start | bytes 3670016 | tf_op jit(solution)/shard_map/while/body/eval_jaxpr/cond/branch_1_fun/all_to_all | solution.py:80
  390.8 3.7 collective-permute-start
  394.5 0.8 copy-start.1

commit v5 on v4

--- a/solution.py
+++ b/solution.py
@@ -36,6 +36,7 @@
 
     route_member = (routes[0][..., None] == expert_ids).astype(jnp.float32)
     expert_local = jnp.sum(route_member, axis=(0, 1, 2))
+    own_expert = ep_index // 2
     own_hot = jnp.sum(jnp.where(expert_ids == hot_expert, expert_local, 0.0))
 
     def expert_rows(flat_rows):
@@ -65,16 +66,11 @@
             normed,
             preferred_element_type=jnp.float32,
         ).astype(jnp.bfloat16)
-        item_count = micro_count * capacity
-        packed = packed.reshape(expert_count, item_count, model_width)
-        count_row = jnp.broadcast_to(
-            jnp.sum(routed, axis=(0, 1))[:, None, None], (expert_count, 1, model_width)
-        ).astype(jnp.bfloat16)
-        send_rows = jnp.repeat(jnp.concatenate([packed, count_row], axis=1), 2, axis=0)
-        recv_all = lax.all_to_all(send_rows, "ep", split_axis=0, concat_axis=0, tiled=True)
-        recv_rows = recv_all[:, :item_count]
-        filled = jnp.sum(recv_all[:, item_count, 0].astype(jnp.float32))
+        packed = packed.reshape(expert_count, micro_count * capacity, model_width)
+        send_rows = jnp.repeat(packed, 2, axis=0)
+        recv_rows = lax.all_to_all(send_rows, "ep", split_axis=0, concat_axis=0, tiled=True)
         sources = recv_rows.shape[0]
+        item_count = recv_rows.shape[1]
         part = expert_rows(recv_rows.reshape(sources * item_count, model_width))
         part = part.reshape(sources, item_count, model_width)
         home_back = lax.all_to_all(part, "ep", split_axis=0, concat_axis=0, tiled=True)
@@ -86,6 +82,8 @@
         routed_sum = jnp.einsum(
             "mect,emcf->mtf", weighting, pair_sum, precision=lax.Precision.HIGHEST
         )
+        expert_total = lax.psum(expert_local, "ep")
+        filled = jnp.sum(jnp.where(expert_ids == own_expert, expert_total, 0.0))
         return ((rows_float + routed_sum).astype(jnp.bfloat16), filled)
 
     route_ids = routes[0]

time: 397 us -> 378 us (0.952)
  waiting for transfers between devices: 316 us -> 280 us
  blocking collectives: 36.4 us -> 56 us
    psum x0 -> x1, blocking collectives: none -> 28.7 us  [apply_layer(): expert_total = lax.psum(expert_local, 'ep')]
    all_to_all x1, waiting for transfers between devices: 21.8 us -> 0.01 us  [apply_layer(): lax.all_to_all(part, 'ep', split_axis=0, concat_axis=0, tiled=True)]
    ppermute x4, waiting for transfers between devices: 294 us -> 280 us  [shifted(): return lax.ppermute(block, axis, route)]
    all_to_all x1, blocking collectives: 36.4 us -> 27.3 us  [apply_layer(): lax.all_to_all(send_rows, 'ep', split_axis=0, concat_axis=0, tiled=True)]
  transfers between devices with their start and end apart: 5 -> 5, of which waited for: 5 -> 4; matrix products, arithmetic and copies ran while one was open for 1% -> 0% of each run, Pallas kernels for 0% -> 0%
where the time goes in v5:
time: 378 us; the launch traced here: 377 us
  waiting for transfers between devices  280 us (74%)
  blocking collectives  56 us (15%)
  matrix products  16.9 us (4%)
  starting transfers between devices  8.76 us (2%)
  other arithmetic  6.7 us (2%)
  local copies, waits for them, and re-layouts  4.09 us (1%)
    ppermute x4, waiting for transfers between devices, shifted(): return lax.ppermute(block, axis, route)  280 us
    psum x1, blocking collectives, apply_layer(): expert_total = lax.psum(expert_local, 'ep')  28.7 us
    all_to_all x1, blocking collectives, apply_layer(): lax.all_to_all(send_rows, 'ep', split_axis=0, concat_axis=0, tiled=True)  27.3 us
    dot_general x1, matrix products, expert_rows(): jnp.dot(activation, down_w, preferred_element_type=jnp.float32)  8.64 us
  transfers between devices with their start and end apart: 5, of which 4 were waited for; matrix products, arithmetic and copies ran while one was open for 0% of the time, Pallas kernels for 0%

profile of v5, /device:TPU:5, one launch (start us, length us, event | category | flops | bytes accessed | tf_op | source)
XLA Modules:
  0.0 376.8 jit_solution(4336074655070428993)
XLA Ops:
  0.6 0.8 convert_reduce_fusion
  1.5 0.7 copy.32
  2.2 371.5 %while.20 = (s32[]{:T(128)}, bf16[4,8,7168]{2,1,0:T(8,128)(2,1)S(1)}, bf16[4,8,7168]{2,1,0:T(8,128)(2,1)S(1)}, f32[]{:T(128)}, s32[]{:T(128)}, /*index=5*/pred[]...) while((s32[]{:T(128)}, ...), condition=%wide.region_12.13_spmd.clone.clone, body=%wide.region_1.12_spmd.clone.clone.sunk | while | flops 2877921280 | bytes 93778304 | solution.py:108
  2.3 1.3 collective-permute-start
  3.6 0.2 select_select_fusion.2
  3.8 2.4 collective-permute-done
  6.3 1.3 collective-permute-start
  7.6 0.2 select_select_fusion.2
  7.8 8.3 %collective-permute-done = bf16[4,8,7168]{2,1,0:T(8,128)(2,1)S(1)} collective-permute-done((bf16[4,8,7168]{2,1,0:T(8,128)(2,1)S(1)}, bf16[4,8,7168]{2,1,0:T(8,128)(2,1)S(1)}, u32[]{:S(2)}, u32[]{:S(2)}) %collective-permute-start) | collective-permute-done | bytes 458784 | tf_op jit(solution)/shard_map/while/body/eval_jaxpr/ppermute | solution.py:13
  16.2 1.3 collective-permute-start
  17.5 0.2 select_select_fusion.2
  17.7 267.4 %collective-permute-done = bf16[4,8,7168]{2,1,0:T(8,128)(2,1)S(1)} collective-permute-done((bf16[4,8,7168]{2,1,0:T(8,128)(2,1)S(1)}, bf16[4,8,7168]{2,1,0:T(8,128)(2,1)S(1)}, u32[]{:S(2)}, u32[]{:S(2)}) %collective-permute-start) | collective-permute-done | bytes 458784 | tf_op jit(solution)/shard_map/while/body/eval_jaxpr/ppermute | solution.py:13
  285.1 84.9 %conditional.4 = (bf16[4,8,7168]{2,1,0:T(8,128)(2,1)S(1)}, f32[]{:T(128)}) conditional(s32[]{:T(128)} %convert_element_type.79, bf16[4,8,7168]{2,1,0:T(8,128)(2,1)S(1)} %broadcast_select_fusion.2, (bf16[4,8,7168]{2,1,0:T(8,128)(2,1)S(1)}, s32[1,4,8,2]{2,1,3,0:T(4,128)S(1)}, s32[4]{0:T(128)S(1)}, f32[1,7168]{1,0:T(1,128)}, bf16[7168,4]{0,1:T(4,128)(2,1)}, ...), branch_computations={%region_2.2_spmd, %region_3.11_spmd} | conditional | flops 2877233152 | bytes 89190456 | solution.py:94
  285.1 0.2 fusion.11
  285.3 2.0 fusion.10
  287.6 0.7 reduce_window_sum.11
  288.3 1.4 fusion.2
  289.8 0.5 copy.27
  290.3 0.3 copy.28
  290.5 0.2 broadcast_in_dim.5
  290.8 27.3 %all_to_all.8 = bf16[8,16,7168]{2,1,0:T(8,128)(2,1)S(1)} all-to-all(bf16[8,16,7168]{2,1,0:T(8,128)(2,1)S(1)} %bitcast.53), channel_id=1, replica_groups=mesh['section'=4,'ep'=8] {'ep'}, dimensions={0} | all-to-all | bytes 3670016 | tf_op jit(solution)/shard_map/while/body/eval_jaxpr/cond/branch_1_fun/all_to_all | solution.py:71
  318.1 1.1 fusion.35
  319.2 8.6 %convolution_convert_fusion = bf16[128,7168]{1,0:T(8,128)(2,1)} fusion(bf16[512,7168]{1,0:T(8,128)(2,1)} %get-tuple-element.322, bf16[128,7168]{1,0:T(8,128)(2,1)S(1)} %bitcast.48, bf16[7168,512]{1,0:T(8,128)(2,1)} %get-tuple-element.321, f32[128,512]{1,0:T(8,128)S(1)} %fusion.35), kind=kOutput, calls=%fused_computation.1 | convolution fusion | flops 1880358912 | bytes 18612224 | tf_op jit(solution)/shard_map/while/body/eval_jaxpr/cond/branch_1_fun/dot_general | solution.py:46
  327.8 3.6 all-to-all-start.1
  331.4 28.7 %psum.6 = f32[4]{0:T(128)S(1)} all-reduce(f32[4]{0:T(128)S(1)} %get-tuple-element.325), channel_id=1, replica_groups=mesh['section'=4,'ep'=8] {'ep'}, use_global_device_ids=true, to_apply=%region_10.9 | all-reduce | flops 4 | bytes 32 | tf_op jit(solution)/shard_map/while/body/eval_jaxpr/cond/branch_1_fun/psum | solution.py:85
  360.1 0.7 fusion.31
  360.8 2.4 reshape.49
  363.2 2.5 fusion.5
  365.7 3.7 fusion.4
  370.0 1.3 collective-permute-start
  371.5 2.2 collective-permute-done
  374.4 0.6 fusion.34
  (26 shorter events, 0.7 us)
Async XLA Ops:
  2.3 3.9 %collective-permute-start = (bf16[4,8,7168]{2,1,0:T(8,128)(2,1)S(1)}, bf16[4,8,7168]{2,1,0:T(8,128)(2,1)S(1)}, u32[]{:S(2)}, u32[]{:S(2)}) collective-permute-start(bf16[4,8,7168]{2,1,0:T(8,128)(2,1)S(1)} %get-tuple-element.614), channel_id=1, source_target_pairs={{0,8},{8,16},{16,24},{1,9},{9,17},{17,25},{2,10},{10,18},{18,26},{... | collective-permute-start | bytes 1376264 | tf_op jit(solution)/shard_map/while/body/eval_jaxpr/ppermute | solution.py:13
  6.3 9.8 %collective-permute-start = (bf16[4,8,7168]{2,1,0:T(8,128)(2,1)S(1)}, bf16[4,8,7168]{2,1,0:T(8,128)(2,1)S(1)}, u32[]{:S(2)}, u32[]{:S(2)}) collective-permute-start(bf16[4,8,7168]{2,1,0:T(8,128)(2,1)S(1)} %get-tuple-element.614), channel_id=1, source_target_pairs={{0,8},{8,16},{16,24},{1,9},{9,17},{17,25},{2,10},{10,18},{18,26},{... | collective-permute-start | bytes 1376264 | tf_op jit(solution)/shard_map/while/body/eval_jaxpr/ppermute | solution.py:13
  16.2 268.9 %collective-permute-start = (bf16[4,8,7168]{2,1,0:T(8,128)(2,1)S(1)}, bf16[4,8,7168]{2,1,0:T(8,128)(2,1)S(1)}, u32[]{:S(2)}, u32[]{:S(2)}) collective-permute-start(bf16[4,8,7168]{2,1,0:T(8,128)(2,1)S(1)} %get-tuple-element.614), channel_id=1, source_target_pairs={{0,8},{8,16},{16,24},{1,9},{9,17},{17,25},{2,10},{10,18},{18,26},{... | collective-permute-start | bytes 1376264 | tf_op jit(solution)/shard_map/while/body/eval_jaxpr/ppermute | solution.py:13
  290.2 27.8 %copy-start = (bf16[7168,512]{1,0:T(8,128)(2,1)S(1)}, bf16[7168,512]{1,0:T(8,128)(2,1)}, u32[]{:S(2)}) copy-start(bf16[7168,512]{1,0:T(8,128)(2,1)} %get-tuple-element.320) | copy-start | bytes 22020100 | tf_op jit(solution)/shard_map/while/body/eval_jaxpr/cond
  327.8 33.0 %all-to-all-start.1 = ((bf16[8,16,7168]{2,1,0:T(8,128)(2,1)}), bf16[8,16,7168]{2,1,0:T(8,128)(2,1)S(1)}, u32[]{:S(2)}, u32[]{:S(2)}) async-start(bf16[8,16,7168]{2,1,0:T(8,128)(2,1)} %bitcast.50), calls=%async_computation.1 | async-start | bytes 3670016 | tf_op jit(solution)/shard_map/while/body/eval_jaxpr/cond/branch_1_fun/all_to_all | solution.py:76
  370.0 3.7 collective-permute-start
  373.7 2.0 copy-start.1
